TPU v7x, 128 devices: a whole 4x4x4 slice. The times are simulated.
128 devices in a mesh: smp: 8 (over x_lo, z), bld: 16 (over y, x_hi, core).
Axes of the slice: x: 4 (x_hi: 2, x_lo: 2; x = x_hi * 2 + x_lo), y: 4, z: 4, core: 2. Of those that a mesh axis runs over, the one named last changes fastest.
Arguments:
- tensor: bfloat16 [4, 8192, 16384], P(None, 'smp', 'bld'), may hold values from -576 to 576
- building_factor: float32 [64, 16384], P(None, 'bld'), may hold values from -144 to 144
- hour_weights: float32 [4, 64], replicated, may hold values from -5 to 5
Outputs:
- sample_factor: float32 [64, 8192], P(None, ('smp', 'bld'))
- building_out: float32 [64, 16384], P(None, ('bld', 'smp'))
- hour_out: float32 [4, 64], replicated
All inputs are finite; a program needn't handle non-finite values.
Results may differ from a plain program's by a relative error of at most 0.008.
Values may be sent and summed in bfloat16 or wider, within the bound.
A program may use at most 64 MiB of HBM per device.

v0:
```python
import math

import jax
import jax.numpy as jnp
from jax import lax
from jax.sharding import PartitionSpec as P

SWEEPS = 5


EPSILON = 1e-06
RIDGE_SHARE = 0.05


def regularized(gram):
    order_size = gram.shape[0]
    return gram + RIDGE_SHARE * jnp.mean(jnp.diagonal(gram)) * jnp.eye(order_size, dtype=gram.dtype)


def solve_rows(gram, right_side):
    lower_factor = jnp.linalg.cholesky(regularized(gram))
    middle = lax.linalg.triangular_solve(lower_factor, right_side, left_side=True, lower=True)
    return lax.linalg.triangular_solve(
        lower_factor, middle, left_side=True, lower=True, transpose_a=True
    )


def finish(unscaled, gram_raw, row_count):
    column_norm = jnp.sqrt(jnp.diagonal(gram_raw) / row_count + EPSILON)
    return (
        unscaled / column_norm[:, None],
        gram_raw / (column_norm[:, None] * column_norm[None, :]),
    )


def hour_gram(hourly):
    return jnp.dot(hourly.T, hourly, precision=lax.Precision.HIGHEST)


def self_gram(unscaled):
    return jnp.dot(unscaled, unscaled.T, precision=lax.Precision.HIGHEST)


def local(tensor, building_factor, hour_weights):
    samples_total = tensor.shape[1] * lax.axis_size("smp")
    buildings_total = tensor.shape[2] * lax.axis_size("bld")
    scale_up = math.sqrt(samples_total * buildings_total)
    hourly = hour_weights / scale_up
    gram_build = lax.psum(self_gram(building_factor), "bld")
    build_low = building_factor.astype(jnp.bfloat16)
    partial_value = jnp.einsum("rj,kij->kri", build_low, tensor, preferred_element_type=jnp.float32)
    sample_out = None
    building_out = None
    for sweep_index in range(SWEEPS):
        sample_terms = jnp.sum(hourly[:, :, None] * partial_value, axis=0)
        sample_rhs = lax.psum(sample_terms, "bld")
        unscaled = solve_rows(gram_build * hour_gram(hourly), sample_rhs)
        gram_raw = lax.psum(self_gram(unscaled), "smp")
        samples_now, gram_sample = finish(unscaled, gram_raw, samples_total)
        sample_low = samples_now.astype(jnp.bfloat16)
        share_width = samples_now.shape[1] // lax.axis_size("bld")
        sample_out = lax.dynamic_slice_in_dim(
            samples_now, lax.axis_index("bld") * share_width, share_width, 1
        )
        mixed = jnp.einsum("ri,kij->krj", sample_low, tensor, preferred_element_type=jnp.float32)
        build_terms = jnp.sum(hourly[:, :, None] * mixed, axis=0)
        build_rhs = lax.psum(build_terms, "smp")
        unscaled = solve_rows(gram_sample * hour_gram(hourly), build_rhs)
        gram_raw = lax.psum(self_gram(unscaled), "bld")
        building_now, gram_build = finish(unscaled, gram_raw, buildings_total)
        build_low = building_now.astype(jnp.bfloat16)
        share_width = building_now.shape[1] // lax.axis_size("smp")
        building_out = lax.dynamic_slice_in_dim(
            building_now, lax.axis_index("smp") * share_width, share_width, 1
        )
        partial_value = jnp.einsum(
            "rj,kij->kri", build_low, tensor, preferred_element_type=jnp.float32
        )
        hour_terms = jnp.sum(sample_low.astype(jnp.float32)[None, :, :] * partial_value, axis=2)
        hour_rhs = lax.psum(hour_terms, ("smp", "bld"))
        hourly = solve_rows(gram_sample * gram_build, hour_rhs.T).T
    return (sample_out, building_out, hourly * scale_up)


def solution(mesh):
    in_specs = (P(None, "smp", "bld"), P(None, "bld"), P())
    out_specs = (P(None, ("smp", "bld")), P(None, ("bld", "smp")), P())
    return jax.shard_map(local, mesh=mesh, in_specs=in_specs, out_specs=out_specs, check_vma=False)
```

profile of v0, /device:TPU:1, one launch (start us, length us, event | category | flops | bytes accessed | tf_op | source)
XLA Modules:
  0.0 2094.5 jit_solution(17855161390660669668)
XLA Ops:
  8.0 6.7 fusion.10
  15.2 65.3 %psum.182 = f32[64,64]{0,1:T(8,128)S(1)} all-reduce(f32[64,64]{0,1:T(8,128)S(1)} %fusion.159), channel_id=1, replica_groups=mesh['smp'=8,'bld'=16] {'bld'}, use_global_device_ids=true, to_apply=%region_0.0 | all-reduce | flops 4096 | bytes 32768 | tf_op jit(solution)/shard_map/psum | solution.py:49
  82.9 5.8 cholesky.239
  90.1 4.9 custom-call.91
  95.0 60.6 %all-reduce.11.cloned.1.call-done = f32[64,1024]{1,0:T(8,128)} async-done(((f32[64,1024]{1,0:T(8,128)}), f32[64,1024]{1,0:T(8,128)}) %all-reduce.11.cloned.1.call-update) | async-done | bytes 262160 | tf_op jit(solution)/shard_map/psum | solution.py:56
  157.7 26.2 %psum.184 = f32[64,64]{0,1:T(8,128)S(1)} all-reduce(f32[64,64]{0,1:T(8,128)S(1)} %fusion.160), channel_id=1, replica_groups=mesh['smp'=8,'bld'=16] {'smp'}, use_global_device_ids=true, to_apply=%region_6.10 | all-reduce | flops 4096 | bytes 32768 | tf_op jit(solution)/shard_map/psum | solution.py:58
  184.8 5.8 fusion.5
  192.8 5.8 cholesky.250
  200.1 4.9 custom-call.93
  205.1 65.8 %all-reduce.13.cloned.1.call-done = f32[64,1024]{1,0:T(8,128)} async-done(((f32[64,1024]{1,0:T(8,128)}), f32[64,1024]{1,0:T(8,128)}) %all-reduce.13.cloned.1.call-update) | async-done | bytes 262160 | tf_op jit(solution)/shard_map/psum | solution.py:67
  273.0 65.3 %psum.186 = f32[64,64]{0,1:T(8,128)S(1)} all-reduce(f32[64,64]{0,1:T(8,128)S(1)} %fusion.161), channel_id=1, replica_groups=mesh['smp'=8,'bld'=16] {'bld'}, use_global_device_ids=true, to_apply=%region_10.14 | all-reduce | flops 4096 | bytes 32768 | tf_op jit(solution)/shard_map/psum | solution.py:69
  341.4 5.8 cholesky.261
  348.6 4.9 custom-call.95
  353.5 6.2 multiply_reduce_fusion.7
  359.6 67.3 %psum.187 = f32[64,4]{0,1:T(4,128)S(1)} all-reduce(f32[64,4]{0,1:T(4,128)S(1)} %bitcast.367), channel_id=1, replica_groups=mesh['smp'=8,'bld'=16] {'smp','bld'}, use_global_device_ids=true, to_apply=%region_13.17 | all-reduce | flops 256 | bytes 2048 | tf_op jit(solution)/shard_map/psum | solution.py:80
  429.7 5.8 cholesky.272
  437.8 4.9 custom-call.97
  442.7 127.8 %all-reduce.15.cloned.1.call-done = f32[64,1024]{1,0:T(8,128)} async-done(((f32[64,1024]{1,0:T(8,128)}), f32[64,1024]{1,0:T(8,128)}) %all-reduce.15.cloned.1.call-update) | async-done | bytes 262160 | tf_op jit(solution)/shard_map/psum | solution.py:56
  572.6 26.5 %psum.189 = f32[64,64]{0,1:T(8,128)S(1)} all-reduce(f32[64,64]{0,1:T(8,128)S(1)} %fusion.162), channel_id=1, replica_groups=mesh['smp'=8,'bld'=16] {'smp'}, use_global_device_ids=true, to_apply=%region_17.23 | all-reduce | flops 4096 | bytes 32768 | tf_op jit(solution)/shard_map/psum | solution.py:58
  599.9 5.8 fusion.6
  607.9 5.8 cholesky.283
  615.2 4.9 custom-call.99
  620.2 65.8 %all-reduce.17.cloned.1.call-done = f32[64,1024]{1,0:T(8,128)} async-done(((f32[64,1024]{1,0:T(8,128)}), f32[64,1024]{1,0:T(8,128)}) %all-reduce.17.cloned.1.call-update) | async-done | bytes 262160 | tf_op jit(solution)/shard_map/psum | solution.py:67
  688.1 64.7 %psum.191 = f32[64,64]{0,1:T(8,128)S(1)} all-reduce(f32[64,64]{0,1:T(8,128)S(1)} %fusion.163), channel_id=1, replica_groups=mesh['smp'=8,'bld'=16] {'bld'}, use_global_device_ids=true, to_apply=%region_21.27 | all-reduce | flops 4096 | bytes 32768 | tf_op jit(solution)/shard_map/psum | solution.py:69
  755.9 5.8 cholesky.294
  763.1 4.9 custom-call.101
  768.0 6.2 multiply_reduce_fusion.5
  774.2 67.5 %psum.192 = f32[64,4]{0,1:T(4,128)S(1)} all-reduce(f32[64,4]{0,1:T(4,128)S(1)} %bitcast.368), channel_id=1, replica_groups=mesh['smp'=8,'bld'=16] {'smp','bld'}, use_global_device_ids=true, to_apply=%region_24.30 | all-reduce | flops 256 | bytes 2048 | tf_op jit(solution)/shard_map/psum | solution.py:80
  844.5 5.8 cholesky.305
  852.6 4.9 custom-call.103
  857.5 127.8 %all-reduce.19.cloned.1.call-done = f32[64,1024]{1,0:T(8,128)} async-done(((f32[64,1024]{1,0:T(8,128)}), f32[64,1024]{1,0:T(8,128)}) %all-reduce.19.cloned.1.call-update) | async-done | bytes 262160 | tf_op jit(solution)/shard_map/psum | solution.py:56
  987.4 26.2 %psum.194 = f32[64,64]{0,1:T(8,128)S(1)} all-reduce(f32[64,64]{0,1:T(8,128)S(1)} %fusion.164), channel_id=1, replica_groups=mesh['smp'=8,'bld'=16] {'smp'}, use_global_device_ids=true, to_apply=%region_28.34 | all-reduce | flops 4096 | bytes 32768 | tf_op jit(solution)/shard_map/psum | solution.py:58
  1014.4 5.8 fusion.7
  1022.4 5.8 cholesky.316
  1029.7 4.9 custom-call.105
  1034.7 65.8 %all-reduce.21.cloned.1.call-done = f32[64,1024]{1,0:T(8,128)} async-done(((f32[64,1024]{1,0:T(8,128)}), f32[64,1024]{1,0:T(8,128)}) %all-reduce.21.cloned.1.call-update) | async-done | bytes 262160 | tf_op jit(solution)/shard_map/psum | solution.py:67
  1102.6 65.2 %psum.196 = f32[64,64]{0,1:T(8,128)S(1)} all-reduce(f32[64,64]{0,1:T(8,128)S(1)} %fusion.165), channel_id=1, replica_groups=mesh['smp'=8,'bld'=16] {'bld'}, use_global_device_ids=true, to_apply=%region_32.38 | all-reduce | flops 4096 | bytes 32768 | tf_op jit(solution)/shard_map/psum | solution.py:69
  1170.8 5.8 cholesky.327
  1178.0 4.9 custom-call.107
  1182.9 6.2 multiply_reduce_fusion.3
  1189.1 67.3 %psum.197 = f32[64,4]{0,1:T(4,128)S(1)} all-reduce(f32[64,4]{0,1:T(4,128)S(1)} %bitcast.369), channel_id=1, replica_groups=mesh['smp'=8,'bld'=16] {'smp','bld'}, use_global_device_ids=true, to_apply=%region_35.41 | all-reduce | flops 256 | bytes 2048 | tf_op jit(solution)/shard_map/psum | solution.py:80
  1259.2 5.8 cholesky.338
  1267.3 4.9 custom-call.109
  1272.2 127.8 %all-reduce.23.cloned.1.call-done = f32[64,1024]{1,0:T(8,128)} async-done(((f32[64,1024]{1,0:T(8,128)}), f32[64,1024]{1,0:T(8,128)}) %all-reduce.23.cloned.1.call-update) | async-done | bytes 262160 | tf_op jit(solution)/shard_map/psum | solution.py:56
  1402.0 26.5 %psum.199 = f32[64,64]{0,1:T(8,128)S(1)} all-reduce(f32[64,64]{0,1:T(8,128)S(1)} %fusion.166), channel_id=1, replica_groups=mesh['smp'=8,'bld'=16] {'smp'}, use_global_device_ids=true, to_apply=%region_39.45 | all-reduce | flops 4096 | bytes 32768 | tf_op jit(solution)/shard_map/psum | solution.py:58
  1429.4 5.8 fusion.8
  1437.4 5.8 cholesky.349
  1444.7 4.9 custom-call.111
  1449.7 65.8 %all-reduce.25.cloned.1.call-done = f32[64,1024]{1,0:T(8,128)} async-done(((f32[64,1024]{1,0:T(8,128)}), f32[64,1024]{1,0:T(8,128)}) %all-reduce.25.cloned.1.call-update) | async-done | bytes 262160 | tf_op jit(solution)/shard_map/psum | solution.py:67
  1517.6 64.7 %psum.201 = f32[64,64]{0,1:T(8,128)S(1)} all-reduce(f32[64,64]{0,1:T(8,128)S(1)} %fusion.167), channel_id=1, replica_groups=mesh['smp'=8,'bld'=16] {'bld'}, use_global_device_ids=true, to_apply=%region_43.49 | all-reduce | flops 4096 | bytes 32768 | tf_op jit(solution)/shard_map/psum | solution.py:69
  1585.4 5.8 cholesky.360
  1592.6 4.9 custom-call.113
  1597.5 6.2 multiply_reduce_fusion.1
  1603.6 67.5 %psum.202 = f32[64,4]{0,1:T(4,128)S(1)} all-reduce(f32[64,4]{0,1:T(4,128)S(1)} %bitcast.370), channel_id=1, replica_groups=mesh['smp'=8,'bld'=16] {'smp','bld'}, use_global_device_ids=true, to_apply=%region_46.52 | all-reduce | flops 256 | bytes 2048 | tf_op jit(solution)/shard_map/psum | solution.py:80
  1673.9 5.8 cholesky.371
  1686.9 127.8 %all-reduce.27.cloned.1.call-done = f32[64,1024]{1,0:T(8,128)} async-done(((f32[64,1024]{1,0:T(8,128)}), f32[64,1024]{1,0:T(8,128)}) %all-reduce.27.cloned.1.call-update) | async-done | bytes 262160 | tf_op jit(solution)/shard_map/psum | solution.py:56
  1816.8 26.2 %psum.204 = f32[64,64]{0,1:T(8,128)S(1)} all-reduce(f32[64,64]{0,1:T(8,128)S(1)} %fusion.168), channel_id=1, replica_groups=mesh['smp'=8,'bld'=16] {'smp'}, use_global_device_ids=true, to_apply=%region_50.56 | all-reduce | flops 4096 | bytes 32768 | tf_op jit(solution)/shard_map/psum | solution.py:58
  1846.2 5.8 cholesky.382
  1852.8 5.7 fusion.9
  1864.7 65.3 %all-reduce.29.cloned.1.call-done = f32[64,1024]{1,0:T(8,128)} async-done(((f32[64,1024]{1,0:T(8,128)}), f32[64,1024]{1,0:T(8,128)}) %all-reduce.29.cloned.1.call-update) | async-done | bytes 262160 | tf_op jit(solution)/shard_map/psum | solution.py:67
  1932.1 65.0 %psum.206 = f32[64,64]{0,1:T(8,128)S(1)} all-reduce(f32[64,64]{0,1:T(8,128)S(1)} %fusion.169), channel_id=1, replica_groups=mesh['smp'=8,'bld'=16] {'bld'}, use_global_device_ids=true, to_apply=%region_54.60 | all-reduce | flops 4096 | bytes 32768 | tf_op jit(solution)/shard_map/psum | solution.py:69
  2000.3 5.8 cholesky.393
  2012.4 6.2 fusion.11
  2018.5 67.3 %psum.207 = f32[64,4]{0,1:T(4,128)S(1)} all-reduce(f32[64,4]{0,1:T(4,128)S(1)} %fusion.11), channel_id=1, replica_groups=mesh['smp'=8,'bld'=16] {'smp','bld'}, use_global_device_ids=true, to_apply=%region_57.63 | all-reduce | flops 256 | bytes 2048 | tf_op jit(solution)/shard_map/psum | solution.py:80
  (237 shorter events, 97.5 us)
Async XLA Ops:
  7.2 73.3 %copy-start.1 = (f32[4,64]{1,0:T(4,128)S(1)}, f32[4,64]{1,0:T(4,128)}, u32[]{:S(2)}) copy-start(f32[4,64]{1,0:T(4,128)} %param.14) | copy-start | bytes 3076
  7.2 7.6 copy-start
  7.2 148.4 %all-reduce.11.cloned.1.call-start = ((), (), s32[]{:S(2)}) async-start(), calls=%async_computation | async-start | bytes 524288 | tf_op jit(solution)/shard_map/psum | solution.py:56
  14.7 256.2 %all-reduce.13.cloned.1.call-start = ((), (), s32[]{:S(2)}) async-start(), calls=%async_computation.1 | async-start | bytes 524288 | tf_op jit(solution)/shard_map/psum | solution.py:67
  199.4 371.1 %all-reduce.15.cloned.1.call-start = ((), (), s32[]{:S(2)}) async-start(), calls=%async_computation.2 | async-start | bytes 524288 | tf_op jit(solution)/shard_map/psum | solution.py:56
  436.5 249.5 %all-reduce.17.cloned.1.call-start = ((), (), s32[]{:S(2)}) async-start(), calls=%async_computation.3 | async-start | bytes 524288 | tf_op jit(solution)/shard_map/psum | solution.py:67
  614.5 370.8 %all-reduce.19.cloned.1.call-start = ((), (), s32[]{:S(2)}) async-start(), calls=%async_computation.4 | async-start | bytes 524288 | tf_op jit(solution)/shard_map/psum | solution.py:56
  851.2 249.2 %all-reduce.21.cloned.1.call-start = ((), (), s32[]{:S(2)}) async-start(), calls=%async_computation.5 | async-start | bytes 524288 | tf_op jit(solution)/shard_map/psum | solution.py:67
  1029.0 371.0 %all-reduce.23.cloned.1.call-start = ((), (), s32[]{:S(2)}) async-start(), calls=%async_computation.6 | async-start | bytes 524288 | tf_op jit(solution)/shard_map/psum | solution.py:56
  1265.9 249.5 %all-reduce.25.cloned.1.call-start = ((), (), s32[]{:S(2)}) async-start(), calls=%async_computation.7 | async-start | bytes 524288 | tf_op jit(solution)/shard_map/psum | solution.py:67
  1443.9 370.8 %all-reduce.27.cloned.1.call-start = ((), (), s32[]{:S(2)}) async-start(), calls=%async_computation.8 | async-start | bytes 524288 | tf_op jit(solution)/shard_map/psum | solution.py:56
  1680.7 249.3 %all-reduce.29.cloned.1.call-start = ((), (), s32[]{:S(2)}) async-start(), calls=%async_computation.9 | async-start | bytes 524288 | tf_op jit(solution)/shard_map/psum | solution.py:67
Sparse Core Ops, SparseCore 0:
  14.8 140.7 all-reduce.10
  199.5 71.3 all-reduce.12
  436.6 133.8 all-reduce.14
  614.6 71.3 all-reduce.16
  851.4 133.8 all-reduce.18
  1029.1 71.3 all-reduce.20
  1266.0 133.8 all-reduce.22
  1444.1 71.3 all-reduce.24
  1680.8 133.8 all-reduce.26
  1858.6 71.3 all-reduce.28
where the time goes:
time: 2100 us; the launch traced here: 2090 us
  waiting for transfers between devices  900 us (43%)
  blocking collectives  859 us (41%)
  other arithmetic  196 us (9%)
  matrix products  90.9 us (4%)
  between operations  25.1 us (1%)
  local copies, waits for them, and re-layouts  22.6 us (1%)
    psum x5, waiting for transfers between devices, local(): sample_rhs = lax.psum(sample_terms, 'bld')  572 us
    psum x5, blocking collectives, local(): hour_rhs = lax.psum(hour_terms, ('smp', 'bld'))  337 us
    psum x5, waiting for transfers between devices, local(): build_rhs = lax.psum(build_terms, 'smp')  328 us
    psum x5, blocking collectives, local(): gram_raw = lax.psum(self_gram(unscaled), 'bld')  325 us
    psum x5, blocking collectives, local(): gram_raw = lax.psum(self_gram(unscaled), 'smp')  132 us
    another operation x45, other arithmetic, solve_rows(): lower_factor = jnp.linalg.cholesky(regularized(gram))  97.7 us
    another operation x30, other arithmetic, solve_rows(): lax.linalg.triangular_solve(lower_factor, middle, left_side=True, lower=T...  83.3 us
    psum x1, blocking collectives, local(): gram_build = lax.psum(self_gram(building_factor), 'bld')  65.3 us
  transfers between devices with their start and end apart: 10, of which 10 were waited for; matrix products, arithmetic and copies ran while one was open for 3% of the time, Pallas kernels for 0%

commit v1 on v0

v1 whole, which is shorter than its diff:
```python
import functools
import math

import jax
import jax.numpy as jnp
from jax import lax
from jax.experimental import pallas as pl
from jax.experimental.pallas import tpu as pltpu
from jax.sharding import PartitionSpec as P

SWEEPS = 5
EPSILON = 1e-06
RIDGE_SHARE = 0.05
HIGHEST = lax.Precision.HIGHEST
MESH = pl.DeviceIdType.MESH
NT = (((1,), (1,)), ((), ()))
NN = (((1,), (0,)), ((), ()))

BLD_STEPS = [
    (dy, dx, dc) for dy in (2, 1, 3, 0) for dx in (1, 0) for dc in (1, 0) if (dy, dx, dc) != (0, 0, 0)
]
SMP_STEPS = [(dx, dz) for dz in (2, 1, 3, 0) for dx in (1, 0) if (dx, dz) != (0, 0)]


def dot32(a, b, dims=NN):
    return lax.dot_general(a, b, dims, precision=HIGHEST, preferred_element_type=jnp.float32)


def dot16(a, b, dims=NN):
    return lax.dot_general(a, b, dims, preferred_element_type=jnp.float32)


def identity(n):
    rows = lax.broadcasted_iota(jnp.int32, (n, n), 0)
    cols = lax.broadcasted_iota(jnp.int32, (n, n), 1)
    return (rows == cols).astype(jnp.float32)


def pack(square):
    half = square.shape[0] // 2
    return jnp.concatenate([square[:half], square[half:]], axis=1)


def unpack(packed):
    half = packed.shape[1] // 2
    return jnp.concatenate([packed[:, :half], packed[:, half:]], axis=0)


def regularized_inverse(gram):
    n = gram.shape[0]
    eye = identity(n)
    mean = jnp.sum(jnp.sum(gram * eye, axis=0, keepdims=True), axis=1, keepdims=True) / n
    scale = 2.0 / ((n + 2 * RIDGE_SHARE) * mean)
    first = scale * (gram + RIDGE_SHARE * mean * eye)
    spread = n / (n + 2 * RIDGE_SHARE)
    t = first
    y = None
    steps = 7
    for step in range(steps):
        spread = spread * spread / (2.0 - spread * spread)
        gain = 1.0 + spread
        factor = gain * (2.0 * eye - t)
        if step == 0:
            y = factor
            t = dot32(t, factor)
        elif step < steps - 1:
            both = dot32(jnp.concatenate([y, t], axis=0), factor)
            y, t = both[:n], both[n:]
        else:
            y = dot32(y, factor)
    residual = eye - dot32(first, y)
    y = y + dot32(y, residual)
    return scale * y


def scales_of(gram_raw, count):
    eye = identity(gram_raw.shape[0])
    diag_row = jnp.sum(gram_raw * eye, axis=0, keepdims=True)
    diag_col = jnp.sum(gram_raw * eye, axis=1, keepdims=True)
    inv_row = 1.0 / jnp.sqrt(diag_row / count + EPSILON)
    inv_col = 1.0 / jnp.sqrt(diag_col / count + EPSILON)
    return inv_row, inv_col


def kernel(
    n_smp, n_bld, samples_total, buildings_total,
    tensor_ref, build_ref, hour_ref,
    sample_out, build_out, hour_out,
    slab, partial, mixed, factor, us_slice, ub_slice,
    gram_build, gram_sample, hour_rows, hour_cols, inv_b_col, inv_s_row, inv_s_col, gram_tmp,
    rs1_send, rs1_recv, ag1_send, ag1_recv, gs_send, gs_recv,
    rs2_send, rs2_recv, ag2_send, ag2_recv, p1_send, p1_recv, p2_send, p2_recv,
    load_sem, send_sems, recv_sems,
):
    hours, n_i, n_j = slab.shape
    rank = build_ref.shape[0]
    scale_up = math.sqrt(samples_total * buildings_total)
    smp = lax.axis_index("smp")
    bld = lax.axis_index("bld")
    core = bld % 2
    x_hi = (bld // 2) % 2
    y = bld // 4
    z = smp % 4
    x_lo = smp // 4

    def bld_peer(step):
        dy, dx, dc = step
        return ((y + dy) % 4) * 4 + ((x_hi + dx) % 2) * 2 + (core + dc) % 2

    def smp_peer(step):
        dx, dz = step
        return ((x_lo + dx) % 2) * 4 + (z + dz) % 4

    bld_peers = [bld_peer(step) for step in BLD_STEPS]
    smp_peers = [smp_peer(step) for step in SMP_STEPS]

    def start_exchange(axis, sem, piece_of, recv):
        peers, me = (bld_peers, bld) if axis == "bld" else (smp_peers, smp)
        for peer in peers:
            pltpu.make_async_remote_copy(
                src_ref=piece_of(peer),
                dst_ref=recv.at[me],
                send_sem=send_sems.at[sem],
                recv_sem=recv_sems.at[sem],
                device_id={axis: peer},
                device_id_type=MESH,
            ).start()

    def finish_exchange(sem, recv):
        others = recv.at[pl.ds(0, recv.shape[0] - 1)]
        done = pltpu.make_async_remote_copy(
            src_ref=others,
            dst_ref=others,
            send_sem=send_sems.at[sem],
            recv_sem=recv_sems.at[sem],
            device_id={"bld": bld_peers[0]},
            device_id_type=MESH,
        )
        done.wait_recv()
        done.wait_send()

    barrier = pltpu.get_barrier_semaphore()
    for peer in bld_peers:
        pl.semaphore_signal(barrier, inc=1, device_id={"bld": peer}, device_id_type=MESH)
    for peer in smp_peers:
        pl.semaphore_signal(barrier, inc=1, device_id={"smp": peer}, device_id_type=MESH)

    def load(k):
        return pltpu.make_async_copy(tensor_ref.at[k], slab.at[k], load_sem.at[k])

    for k in range(hours):
        load(k).start()

    tile = 512

    def project(k):
        for i in range(0, n_i, tile):
            partial[k, :, i : i + tile] = dot16(factor[...], slab[k, i : i + tile, :], NT)

    def mix(k):
        for j in range(0, n_j, tile):
            mixed[k, :, j : j + tile] = dot16(factor[...], slab[k, :, j : j + tile], NN)

    def share_start(gram, hour_terms):
        gram_tmp[...] = gram
        rows = rank // n_smp
        mine = gram_tmp[pl.ds(pl.multiple_of(smp * rows, rows), rows), :]
        message = jnp.concatenate([mine, hour_terms], axis=1)
        p1_send[...] = message
        p1_recv[bld] = message
        start_exchange("bld", 5, lambda peer: p1_send, p1_recv)

    def share_finish():
        finish_exchange(5, p1_recv)
        total = p1_recv[0]
        for b in range(1, n_bld):
            total = total + p1_recv[b]
        p2_send[...] = total
        p2_recv[smp] = total
        start_exchange("smp", 6, lambda peer: p2_send, p2_recv)
        finish_exchange(6, p2_recv)
        gram = p2_recv[...].reshape(rank, 2 * rank)[:, :rank]
        hour_sum = p2_recv[0][:, rank:]
        for s in range(1, n_smp):
            hour_sum = hour_sum + p2_recv[s][:, rank:]
        return gram, hour_sum

    pad = hour_rows.shape[0]
    rows_k = lax.broadcasted_iota(jnp.int32, (pad, hours * 128), 0)
    lanes_k = lax.broadcasted_iota(jnp.int32, (pad, hours * 128), 1)
    pick = (rows_k == lanes_k // 128).astype(jnp.float32)

    hour_rows[...] = jnp.zeros_like(hour_rows)
    hour_rows[0:hours, :] = hour_ref[...] / scale_up
    hour_cols[...] = dot32(identity(rank), hour_rows[...], NT)
    inv_b_col[...] = jnp.ones_like(inv_b_col)
    start_factor = build_ref[...]
    factor[...] = start_factor.astype(jnp.bfloat16)
    gram0 = dot32(start_factor, start_factor, NT)

    pl.semaphore_wait(barrier, n_bld + n_smp - 2)
    share_start(gram0, jnp.zeros((rank // n_smp, rank), jnp.float32))
    for k in range(hours):
        load(k).wait()
        project(k)
    gram, _ = share_finish()
    gram_build[...] = gram

    @pl.loop(0, SWEEPS)
    def _(sweep):
        gram_hour = dot32(hour_cols[...], hour_rows[...])

        half = rank // 2
        lane = lax.broadcasted_iota(jnp.int32, (half, 128), 1)
        low_lane = lane < 64
        cols = [
            jnp.broadcast_to(hour_cols[:, k : k + 1] * inv_b_col[:, 0:1], (rank, 128))
            for k in range(hours)
        ]
        for m in range(n_bld // 2):
            block = cols[0] * partial[0, :, m * 128 : (m + 1) * 128]
            for k in range(1, hours):
                block = block + cols[k] * partial[k, :, m * 128 : (m + 1) * 128]
            top, low = block[:half], block[half:]
            rs1_send[2 * m] = jnp.where(low_lane, top, pltpu.roll(low, 64, 1)).astype(rs1_send.dtype)
            rs1_send[2 * m + 1] = jnp.where(low_lane, pltpu.roll(top, 64, 1), low).astype(rs1_send.dtype)
        rs1_recv[bld] = rs1_send[bld]
        start_exchange("bld", 0, lambda peer: rs1_send.at[peer], rs1_recv)
        inverse = regularized_inverse(gram_build[...] * gram_hour)
        finish_exchange(0, rs1_recv)
        total = rs1_recv[0].astype(jnp.float32)
        for b in range(1, n_bld):
            total = total + rs1_recv[b].astype(jnp.float32)
        unscaled = dot32(inverse, unpack(total))
        us_slice[...] = unscaled
        message = pack(unscaled).astype(jnp.bfloat16)
        ag1_send[...] = message
        ag1_recv[bld] = message
        start_exchange("bld", 1, lambda peer: ag1_send, ag1_recv)
        finish_exchange(1, ag1_recv)
        for m in range(n_bld // 2):
            even = ag1_recv[2 * m].astype(jnp.float32)
            odd = ag1_recv[2 * m + 1].astype(jnp.float32)
            top = jnp.where(low_lane, even, pltpu.roll(odd, 64, 1))
            low = jnp.where(low_lane, pltpu.roll(even, 64, 1), odd)
            factor[0:half, m * 128 : (m + 1) * 128] = top.astype(jnp.bfloat16)
            factor[half:rank, m * 128 : (m + 1) * 128] = low.astype(jnp.bfloat16)

        gram_part = pack(dot16(factor[...], factor[...], NT))
        gs_send[...] = gram_part
        gs_recv[smp] = gram_part
        start_exchange("smp", 2, lambda peer: gs_send, gs_recv)

        @pl.loop(0, hours)
        def _(k):
            mix(k)

        cols = [jnp.broadcast_to(hour_cols[:, k : k + 1], (rank, 128)) for k in range(hours)]
        for s in range(n_smp):
            block = cols[0] * mixed[0, :, s * 128 : (s + 1) * 128]
            for k in range(1, hours):
                block = block + cols[k] * mixed[k, :, s * 128 : (s + 1) * 128]
            rs2_send[s] = block.astype(rs2_send.dtype)
        rs2_recv[smp] = rs2_send[smp]
        start_exchange("smp", 3, lambda peer: rs2_send.at[peer], rs2_recv)

        finish_exchange(2, gs_recv)
        gram_raw = gs_recv[0]
        for s in range(1, n_smp):
            gram_raw = gram_raw + gs_recv[s]
        gram_raw = unpack(gram_raw)
        inv_row, inv_col = scales_of(gram_raw, samples_total)
        inv_s_row[...] = jnp.broadcast_to(inv_row, inv_s_row.shape)
        inv_s_col[...] = jnp.broadcast_to(inv_col, inv_s_col.shape)
        gram_sample[...] = gram_raw * (inv_col * inv_row)
        inverse = regularized_inverse(gram_sample[...] * gram_hour) * inv_row

        finish_exchange(3, rs2_recv)
        total = rs2_recv[0].astype(jnp.float32)
        for s in range(1, n_smp):
            total = total + rs2_recv[s].astype(jnp.float32)
        unscaled = dot32(inverse, total)
        ub_slice[...] = unscaled
        message = unscaled.astype(jnp.bfloat16)
        ag2_send[...] = message
        ag2_recv[smp] = message
        start_exchange("smp", 4, lambda peer: ag2_send, ag2_recv)
        finish_exchange(4, ag2_recv)
        for s in range(n_smp):
            factor[:, s * 128 : (s + 1) * 128] = ag2_recv[s]

        sums = []
        for k in range(hours):
            acc = jnp.zeros((rank, 128), jnp.float32)
            for s in range(n_smp):
                acc = acc + mixed[k, :, s * 128 : (s + 1) * 128] * ag2_recv[s].astype(jnp.float32)
            sums.append(acc)
        hour_terms = dot32(pick, jnp.concatenate(sums, axis=1), NT)
        share_start(dot16(factor[...], factor[...], NT), hour_terms)

        @pl.loop(0, hours)
        def _(k):
            project(k)

        gram_raw, hour_sum = share_finish()
        inv_row, inv_col = scales_of(gram_raw, buildings_total)
        inv_b_col[...] = jnp.broadcast_to(inv_col, inv_b_col.shape)
        gram_build[...] = gram_raw * (inv_col * inv_row)
        hour_rhs = hour_sum * (inv_row * inv_s_row[0:1, :])
        inverse = regularized_inverse(gram_sample[...] * gram_build[...])
        hour_rows[...] = dot32(hour_rhs, inverse)
        hour_cols[...] = dot32(inverse, hour_rhs, NT)

    sample_out[...] = us_slice[...] * inv_s_col[:, 0:1]
    build_out[...] = ub_slice[...] * inv_b_col[:, 0:1]
    hour_out[...] = hour_rows[0:hours, :] * scale_up


def local(tensor, building_factor, hour_weights):
    n_smp = lax.axis_size("smp")
    n_bld = lax.axis_size("bld")
    hours, n_i, n_j = tensor.shape
    rank = building_factor.shape[0]
    assert (n_smp, n_bld, rank, hours) == (8, 16, 64, 4)
    i_share, j_share = n_i // n_bld, n_j // n_smp
    assert (i_share, j_share) == (64, 128)
    f32, bf16 = jnp.float32, jnp.bfloat16
    body = functools.partial(kernel, n_smp, n_bld, n_i * n_smp, n_j * n_bld)
    vmem = pl.BlockSpec(memory_space=pltpu.VMEM)
    pad = 8
    return pl.pallas_call(
        body,
        out_shape=(
            jax.ShapeDtypeStruct((rank, i_share), f32),
            jax.ShapeDtypeStruct((rank, j_share), f32),
            jax.ShapeDtypeStruct((hours, rank), f32),
        ),
        in_specs=[pl.BlockSpec(memory_space=pl.ANY), vmem, vmem],
        out_specs=(vmem, vmem, vmem),
        scratch_shapes=[
            pltpu.VMEM((hours, n_i, n_j), bf16),
            pltpu.VMEM((hours, rank, n_i), f32),
            pltpu.VMEM((hours, rank, n_j), f32),
            pltpu.VMEM((rank, n_j), bf16),
            pltpu.VMEM((rank, i_share), f32),
            pltpu.VMEM((rank, j_share), f32),
            pltpu.VMEM((rank, rank), f32),
            pltpu.VMEM((rank, rank), f32),
            pltpu.VMEM((pad, rank), f32),
            pltpu.VMEM((rank, pad), f32),
            pltpu.VMEM((rank, pad), f32),
            pltpu.VMEM((pad, rank), f32),
            pltpu.VMEM((rank, pad), f32),
            pltpu.VMEM((rank, rank), f32),
            pltpu.VMEM((n_bld, rank // 2, 2 * i_share), bf16),
            pltpu.VMEM((n_bld, rank // 2, 2 * i_share), bf16),
            pltpu.VMEM((rank // 2, 2 * i_share), bf16),
            pltpu.VMEM((n_bld, rank // 2, 2 * i_share), bf16),
            pltpu.VMEM((rank // 2, 2 * rank), f32),
            pltpu.VMEM((n_smp, rank // 2, 2 * rank), f32),
            pltpu.VMEM((n_smp, rank, j_share), bf16),
            pltpu.VMEM((n_smp, rank, j_share), bf16),
            pltpu.VMEM((rank, j_share), bf16),
            pltpu.VMEM((n_smp, rank, j_share), bf16),
            pltpu.VMEM((rank // n_smp, 2 * rank), f32),
            pltpu.VMEM((n_bld, rank // n_smp, 2 * rank), f32),
            pltpu.VMEM((rank // n_smp, 2 * rank), f32),
            pltpu.VMEM((n_smp, rank // n_smp, 2 * rank), f32),
            pltpu.SemaphoreType.DMA((hours,)),
            pltpu.SemaphoreType.DMA((7,)),
            pltpu.SemaphoreType.DMA((7,)),
        ],
        compiler_params=pltpu.CompilerParams(
            collective_id=0, has_side_effects=True, vmem_limit_bytes=40 * 1024 * 1024
        ),
        name="als_sweeps",
    )(tensor, building_factor, hour_weights)


def solution(mesh):
    in_specs = (P(None, "smp", "bld"), P(None, "bld"), P())
    out_specs = (P(None, ("smp", "bld")), P(None, ("bld", "smp")), P())
    return jax.shard_map(local, mesh=mesh, in_specs=in_specs, out_specs=out_specs, check_vma=False)
```

time: 2100 us -> 186 us (0.09)
  waiting for transfers between devices: 900 us -> 0 us
  blocking collectives: 859 us -> 0 us
  other arithmetic: 196 us -> 0 us
  Pallas kernels: 0 us -> 178 us
  matrix products: 90.9 us -> 0 us
  between operations: 25.1 us -> 0.65 us
    psum x10 -> x0, waiting for transfers between devices: 900 us -> none  [the longest x5 572 us: local(): sample_rhs = lax.psum(sample_terms, 'bld')]
    psum x16 -> x0, blocking collectives: 859 us -> none  [the longest x5 337 us: local(): hour_rhs = lax.psum(hour_terms, ('smp', 'bld'))]
    another operation x75 -> x0, other arithmetic: 181 us -> none  [the longest x45 97.7 us: solve_rows(): lower_factor = jnp.linalg.cholesky(regularized(gram))]
    pallas_call x0 -> x1, Pallas kernels: none -> 178 us  [local(): pl.pallas_call(body, out_shape=(jax.ShapeDtypeStruct((rank, i_share), f32...]
    dot_general x27 -> x0, matrix products: 71.6 us -> none  [the longest x6 37.6 us: local(): jnp.einsum('rj,kij->kri', build_low, tensor, preferred_element_type=jnp.f...]
  transfers between devices with their start and end apart: 10 -> 0, of which waited for: 10 -> 0; matrix products, arithmetic and copies ran while one was open for 3% -> 0% of each run, Pallas kernels for 0% -> 0%
where the time goes in v1:
time: 186 us
  Pallas kernels  178 us (96%)
  local copies, waits for them, and re-layouts  6.81 us (4%)
    pallas_call x1, Pallas kernels, local(): pl.pallas_call(body, out_shape=(jax.ShapeDtypeStruct((rank, i_share), f32...  178 us
    unnamed x9, local copies, waits for them, and re-layouts  6.81 us

profile of v1, /device:TPU:1, one launch (start us, length us, event | category | flops | bytes accessed | tf_op | source)
XLA Modules:
  0.0 185.5 jit_solution(8318557929700901494)
XLA Ops:
  0.6 0.0 copy-start
  0.6 3.4 %copy-done = bf16[4,1024,1024]{2,1,0:T(8,128)(2,1)S(1)} copy-done((bf16[4,1024,1024]{2,1,0:T(8,128)(2,1)S(1)}, bf16[4,1024,1024]{2,1,0:T(8,128)(2,1)}, u32[]{:S(2)}) %copy-start) | copy-done | bytes 8388632
  4.0 0.0 copy-start.1
  4.0 0.9 copy-done.1
  5.0 0.0 copy-start.2
  5.0 0.7 copy-done.2
  5.6 178.1 %als_sweeps.1 = (f32[64,64]{1,0:T(8,128)S(1)}, f32[64,128]{1,0:T(8,128)S(1)}, f32[4,64]{1,0:T(4,128)S(1)}) custom-call(bf16[4,1024,1024]{2,1,0:T(8,128)(2,1)S(1)} %copy-done, f32[64,1024]{1,0:T(8,128)S(1)} %copy-done.1, f32[4,64]{1,0:T(4,128)S(1)} %copy-done.2), custom_call_target="tpu_custom_call" | custom-call | tf_op jit(solution)/shard_map/als_sweeps/pallas_call | solution.py:331
  183.7 0.6 copy.9
  184.4 0.6 copy.10
  185.0 0.6 copy.11
Async XLA Ops:
  0.6 3.4 %copy-start = (bf16[4,1024,1024]{2,1,0:T(8,128)(2,1)S(1)}, bf16[4,1024,1024]{2,1,0:T(8,128)(2,1)}, u32[]{:S(2)}) copy-start(bf16[4,1024,1024]{2,1,0:T(8,128)(2,1)} %tensor_ref.1) | copy-start | bytes 25165828
  4.0 0.9 copy-start.1
  5.0 0.7 copy-start.2

commit v2 on v1

v2 whole, which is shorter than its diff:
```python
import functools
import math

import jax
import jax.numpy as jnp
from jax import lax
from jax.experimental import pallas as pl
from jax.experimental.pallas import tpu as pltpu
from jax.sharding import PartitionSpec as P

SWEEPS = 5
EPSILON = 1e-06
RIDGE_SHARE = 0.05
HIGHEST = lax.Precision.HIGHEST
MESH = pl.DeviceIdType.MESH
NT = (((1,), (1,)), ((), ()))
NN = (((1,), (0,)), ((), ()))

BLD_STEPS = [
    (dy, dx, dc) for dy in (2, 1, 3, 0) for dx in (1, 0) for dc in (1, 0) if (dy, dx, dc) != (0, 0, 0)
]
SMP_STEPS = [(dx, dz) for dz in (2, 1, 3, 0) for dx in (1, 0) if (dx, dz) != (0, 0)]


def dot32(a, b, dims=NN):
    return lax.dot_general(a, b, dims, precision=HIGHEST, preferred_element_type=jnp.float32)


def dot16(a, b, dims=NN):
    return lax.dot_general(a, b, dims, preferred_element_type=jnp.float32)


def identity(n):
    rows = lax.broadcasted_iota(jnp.int32, (n, n), 0)
    cols = lax.broadcasted_iota(jnp.int32, (n, n), 1)
    return (rows == cols).astype(jnp.float32)


def pack(square):
    half = square.shape[0] // 2
    return jnp.concatenate([square[:half], square[half:]], axis=1)


def unpack(packed):
    half = packed.shape[1] // 2
    return jnp.concatenate([packed[:, :half], packed[:, half:]], axis=0)


def regularized_inverse(gram):
    n = gram.shape[0]
    eye = identity(n)
    mean = jnp.sum(jnp.sum(gram * eye, axis=0, keepdims=True), axis=1, keepdims=True) / n
    scale = 2.0 / ((n + 2 * RIDGE_SHARE) * mean)
    t = scale * (gram + RIDGE_SHARE * mean * eye)
    y = None
    spread = n / (n + 2 * RIDGE_SHARE)
    steps = 8
    for step in range(steps):
        spread = spread * spread / (2.0 - spread * spread)
        gain = 1.0 + spread
        factor = gain * (2.0 * eye - t)
        if step == 0:
            y = factor
            t = dot32(t, factor)
        elif step < steps - 1:
            both = dot32(jnp.concatenate([y, t], axis=0), factor)
            y, t = both[:n], both[n:]
        else:
            y = dot32(y, factor)
    return scale * y


def three_parts(x):
    high = x.astype(jnp.bfloat16)
    rest = x - high.astype(jnp.float32)
    middle = rest.astype(jnp.bfloat16)
    low = (rest - middle.astype(jnp.float32)).astype(jnp.bfloat16)
    return jnp.concatenate([high, middle, low], axis=0)


def scales_of(gram_raw, count):
    eye = identity(gram_raw.shape[0])
    diag_row = jnp.sum(gram_raw * eye, axis=0, keepdims=True)
    diag_col = jnp.sum(gram_raw * eye, axis=1, keepdims=True)
    inv_row = 1.0 / jnp.sqrt(diag_row / count + EPSILON)
    inv_col = 1.0 / jnp.sqrt(diag_col / count + EPSILON)
    return inv_row, inv_col


RS1, AG1, GS, RS2, AG2, GB, P1, P2, COUNT = 0, 4, 8, 9, 10, 11, 12, 13, 14


def kernel(
    n_smp, n_bld, samples_total, buildings_total,
    tensor_ref, build_ref, hour_ref,
    sample_out, build_out, hour_out,
    slab, mixed, factor, s_slice, ub_slice,
    gram_build, gram_sample, inv_sample, hour_rows, hour_cols, inv_b_col, inv_s_row, inv_s_col,
    rs1_send, rs1_recv, ag1_send, ag1_recv, gs_send, gs_recv,
    rs2_send, rs2_recv, ag2_send, ag2_recv, gb_send, gb_recv, p1_send, p1_recv, p2_send, p2_recv,
    load_sem, send_sems, recv_sems,
):
    hours, n_i, n_j = slab.shape
    rank = build_ref.shape[0]
    half = rank // 2
    scale_up = math.sqrt(samples_total * buildings_total)
    smp = lax.axis_index("smp")
    bld = lax.axis_index("bld")
    core = bld % 2
    x_hi = (bld // 2) % 2
    y = bld // 4
    z = smp % 4
    x_lo = smp // 4

    def bld_peer(step):
        dy, dx, dc = step
        return ((y + dy) % 4) * 4 + ((x_hi + dx) % 2) * 2 + (core + dc) % 2

    def smp_peer(step):
        dx, dz = step
        return ((x_lo + dx) % 2) * 4 + (z + dz) % 4

    bld_peers = [bld_peer(step) for step in BLD_STEPS]
    smp_peers = [smp_peer(step) for step in SMP_STEPS]

    def start_exchange(axis, piece_of, place, sem_of):
        peers, steps = (bld_peers, BLD_STEPS) if axis == "bld" else (smp_peers, SMP_STEPS)
        for peer, step in zip(peers, steps):
            pltpu.make_async_remote_copy(
                src_ref=piece_of(peer),
                dst_ref=place,
                send_sem=send_sems.at[sem_of(step)],
                recv_sem=recv_sems.at[sem_of(step)],
                device_id={axis: peer},
                device_id_type=MESH,
            ).start()

    def finish_exchange(sem, pieces):
        done = pltpu.make_async_remote_copy(
            src_ref=pieces,
            dst_ref=pieces,
            send_sem=send_sems.at[sem],
            recv_sem=recv_sems.at[sem],
            device_id={"bld": bld_peers[0]},
            device_id_type=MESH,
        )
        done.wait_recv()
        done.wait_send()

    barrier = pltpu.get_barrier_semaphore()
    for peer in bld_peers:
        pl.semaphore_signal(barrier, inc=1, device_id={"bld": peer}, device_id_type=MESH)
    for peer in smp_peers:
        pl.semaphore_signal(barrier, inc=1, device_id={"smp": peer}, device_id_type=MESH)

    def load(k):
        return pltpu.make_async_copy(tensor_ref.at[k], slab.at[k], load_sem.at[k])

    for k in range(hours):
        load(k).start()

    lane = lax.broadcasted_iota(jnp.int32, (half, 128), 1)
    low_lane = lane < 64
    tile = 512

    def project(k):
        for i in range(0, n_i, tile):
            block = dot16(factor[...], slab[k, i : i + tile, :], NT)
            for m in range(tile // 128):
                top, low = block[:half, m * 128 : (m + 1) * 128], block[half:, m * 128 : (m + 1) * 128]
                b = 2 * (i // 128 + m)
                rs1_send[k, b] = jnp.where(low_lane, top, pltpu.roll(low, 64, 1)).astype(rs1_send.dtype)
                rs1_send[k, b + 1] = jnp.where(low_lane, pltpu.roll(top, 64, 1), low).astype(rs1_send.dtype)
        rs1_recv[k, bld] = rs1_send[k, bld]
        start_exchange("bld", lambda peer: rs1_send.at[k, peer], rs1_recv.at[k, bld], lambda step: RS1 + k)

    def build_gram_start(gram):
        message = pack(gram)
        gb_send[...] = message
        gb_recv[bld] = message
        start_exchange("bld", lambda peer: gb_send, gb_recv.at[bld], lambda step: GB)

    def build_gram_finish():
        finish_exchange(GB, gb_recv.at[pl.ds(0, n_bld - 1)])
        total = gb_recv[0]
        for b in range(1, n_bld):
            total = total + gb_recv[b]
        return unpack(total)

    pad = hour_rows.shape[0]
    rows_k = lax.broadcasted_iota(jnp.int32, (pad, hours * 128), 0)
    lanes_k = lax.broadcasted_iota(jnp.int32, (pad, hours * 128), 1)
    pick = (rows_k == lanes_k // 128).astype(jnp.float32)

    hour_rows[...] = jnp.zeros_like(hour_rows)
    hour_rows[0:hours, :] = hour_ref[...] / scale_up
    hour_cols[...] = dot32(identity(rank), hour_rows[...], NT)
    inv_b_col[...] = jnp.ones_like(inv_b_col)
    start_factor = build_ref[...]
    factor[...] = start_factor.astype(jnp.bfloat16)
    gram0 = dot32(start_factor, start_factor, NT)

    pl.semaphore_wait(barrier, n_bld + n_smp - 2)
    build_gram_start(gram0)
    for k in range(hours):
        load(k).wait()
        project(k)
    gram_build[...] = build_gram_finish()

    @pl.loop(0, SWEEPS)
    def _(sweep):
        for k in range(hours):
            finish_exchange(RS1 + k, rs1_recv.at[k, pl.ds(0, n_bld - 1)])
        right = None
        for k in range(hours):
            col = hour_cols[:, k : k + 1] * inv_b_col[:, 0:1]
            both = jnp.where(
                low_lane,
                jnp.broadcast_to(col[:half], (half, 128)),
                jnp.broadcast_to(col[half:], (half, 128)),
            )
            total = rs1_recv[k, 0].astype(jnp.float32)
            for b in range(1, n_bld):
                total = total + rs1_recv[k, b].astype(jnp.float32)
            right = both * total if right is None else right + both * total
        s_slice[...] = right
        message = right.astype(jnp.bfloat16)
        ag1_send[...] = message
        ag1_recv[bld] = message
        start_exchange("bld", lambda peer: ag1_send, ag1_recv.at[bld], lambda step: AG1 + step[0])

        gram_hour = dot32(hour_cols[...], hour_rows[...])
        inverse = regularized_inverse(gram_build[...] * gram_hour)
        inv_sample[...] = inverse
        parts = three_parts(inverse)

        for order, dy in enumerate((0, 1, 3, 2)):
            chunk = (y - dy + 4) % 4
            first = chunk * 4
            finish_exchange(AG1 + dy, ag1_recv.at[pl.ds(0, 3 if dy == 0 else 4)])
            for m in range(2):
                even = ag1_recv[first + 2 * m].astype(jnp.float32)
                odd = ag1_recv[first + 2 * m + 1].astype(jnp.float32)
                top = jnp.where(low_lane, even, pltpu.roll(odd, 64, 1))
                low = jnp.where(low_lane, pltpu.roll(even, 64, 1), odd)
                columns = jnp.concatenate([top, low], axis=0).astype(jnp.bfloat16)
                solved = dot16(parts, columns)
                solved = solved[:rank] + (solved[rank : 2 * rank] + solved[2 * rank :])
                where = pl.multiple_of(chunk * 256 + m * 128, 128)
                factor[:, pl.ds(where, 128)] = solved.astype(jnp.bfloat16)
            rows = pl.ds(pl.multiple_of(chunk * 256, 256), 256)
            if order == 3:
                gram_part = pack(dot16(factor[...], factor[...], NT))
                gs_send[...] = gram_part
                gs_recv[smp] = gram_part
                start_exchange("smp", lambda peer: gs_send, gs_recv.at[smp], lambda step: GS)
            for k in range(hours):
                for j in range(0, n_j, tile):
                    block = dot16(factor[:, rows], slab[k, rows, j : j + tile])
                    if order == 0:
                        mixed[k, :, j : j + tile] = block
                    else:
                        mixed[k, :, j : j + tile] += block

        cols = [jnp.broadcast_to(hour_cols[:, k : k + 1], (rank, 128)) for k in range(hours)]
        for s in range(n_smp):
            block = cols[0] * mixed[0, :, s * 128 : (s + 1) * 128]
            for k in range(1, hours):
                block = block + cols[k] * mixed[k, :, s * 128 : (s + 1) * 128]
            rs2_send[s] = block.astype(rs2_send.dtype)
        rs2_recv[smp] = rs2_send[smp]
        start_exchange("smp", lambda peer: rs2_send.at[peer], rs2_recv.at[smp], lambda step: RS2)

        finish_exchange(GS, gs_recv.at[pl.ds(0, n_smp - 1)])
        gram_raw = gs_recv[0]
        for s in range(1, n_smp):
            gram_raw = gram_raw + gs_recv[s]
        gram_raw = unpack(gram_raw)
        inv_row, inv_col = scales_of(gram_raw, samples_total)
        inv_s_row[...] = jnp.broadcast_to(inv_row, inv_s_row.shape)
        inv_s_col[...] = jnp.broadcast_to(inv_col, inv_s_col.shape)
        gram_sample[...] = gram_raw * (inv_col * inv_row)
        inverse = regularized_inverse(gram_sample[...] * gram_hour) * inv_row

        finish_exchange(RS2, rs2_recv.at[pl.ds(0, n_smp - 1)])
        total = rs2_recv[0].astype(jnp.float32)
        for s in range(1, n_smp):
            total = total + rs2_recv[s].astype(jnp.float32)
        unscaled = dot32(inverse, total)
        ub_slice[...] = unscaled
        message = unscaled.astype(jnp.bfloat16)
        ag2_send[...] = message
        ag2_recv[smp] = message
        start_exchange("smp", lambda peer: ag2_send, ag2_recv.at[smp], lambda step: AG2)
        finish_exchange(AG2, ag2_recv.at[pl.ds(0, n_smp - 1)])

        sums = []
        for k in range(hours):
            acc = jnp.zeros((rank, 128), jnp.float32)
            for s in range(n_smp):
                acc = acc + mixed[k, :, s * 128 : (s + 1) * 128] * ag2_recv[s].astype(jnp.float32)
            sums.append(acc)
        hour_terms = dot32(pick, jnp.concatenate(sums, axis=1), NT)
        message = jnp.concatenate([hour_terms, jnp.zeros_like(hour_terms)], axis=1)
        p1_send[...] = message
        p1_recv[bld] = message
        start_exchange("bld", lambda peer: p1_send, p1_recv.at[bld], lambda step: P1)
        for s in range(n_smp):
            factor[:, s * 128 : (s + 1) * 128] = ag2_recv[s]
        build_gram_start(dot16(factor[...], factor[...], NT))

        @pl.when(sweep < SWEEPS - 1)
        def _():
            for k in range(hours):
                project(k)

        finish_exchange(P1, p1_recv.at[pl.ds(0, n_bld - 1)])
        total = p1_recv[0]
        for b in range(1, n_bld):
            total = total + p1_recv[b]
        p2_send[...] = total
        p2_recv[smp] = total
        start_exchange("smp", lambda peer: p2_send, p2_recv.at[smp], lambda step: P2)

        gram_raw = build_gram_finish()
        inv_row, inv_col = scales_of(gram_raw, buildings_total)
        inv_b_col[...] = jnp.broadcast_to(inv_col, inv_b_col.shape)
        gram_build[...] = gram_raw * (inv_col * inv_row)
        inverse = regularized_inverse(gram_sample[...] * gram_build[...])

        finish_exchange(P2, p2_recv.at[pl.ds(0, n_smp - 1)])
        hour_sum = p2_recv[0]
        for s in range(1, n_smp):
            hour_sum = hour_sum + p2_recv[s]
        hour_rhs = hour_sum[:, :rank] * (inv_row * inv_s_row[0:1, :])
        hour_cols[...] = dot32(inverse, hour_rhs, NT)
        hour_rows[...] = dot32(hour_rhs, inverse)

    sample_out[...] = dot32(inv_sample[...], unpack(s_slice[...])) * inv_s_col[:, 0:1]
    build_out[...] = ub_slice[...] * inv_b_col[:, 0:1]
    hour_out[...] = hour_rows[0:hours, :] * scale_up


def local(tensor, building_factor, hour_weights):
    n_smp = lax.axis_size("smp")
    n_bld = lax.axis_size("bld")
    hours, n_i, n_j = tensor.shape
    rank = building_factor.shape[0]
    assert (n_smp, n_bld, rank, hours) == (8, 16, 64, 4)
    i_share, j_share = n_i // n_bld, n_j // n_smp
    assert (i_share, j_share) == (64, 128)
    f32, bf16 = jnp.float32, jnp.bfloat16
    body = functools.partial(kernel, n_smp, n_bld, n_i * n_smp, n_j * n_bld)
    vmem = pl.BlockSpec(memory_space=pltpu.VMEM)
    pad = 8
    return pl.pallas_call(
        body,
        out_shape=(
            jax.ShapeDtypeStruct((rank, i_share), f32),
            jax.ShapeDtypeStruct((rank, j_share), f32),
            jax.ShapeDtypeStruct((hours, rank), f32),
        ),
        in_specs=[pl.BlockSpec(memory_space=pl.ANY), vmem, vmem],
        out_specs=(vmem, vmem, vmem),
        scratch_shapes=[
            pltpu.VMEM((hours, n_i, n_j), bf16),
            pltpu.VMEM((hours, rank, n_j), f32),
            pltpu.VMEM((rank, n_j), bf16),
            pltpu.VMEM((rank // 2, 2 * i_share), f32),
            pltpu.VMEM((rank, j_share), f32),
            pltpu.VMEM((rank, rank), f32),
            pltpu.VMEM((rank, rank), f32),
            pltpu.VMEM((rank, rank), f32),
            pltpu.VMEM((pad, rank), f32),
            pltpu.VMEM((rank, pad), f32),
            pltpu.VMEM((rank, pad), f32),
            pltpu.VMEM((pad, rank), f32),
            pltpu.VMEM((rank, pad), f32),
            pltpu.VMEM((hours, n_bld, rank // 2, 2 * i_share), bf16),
            pltpu.VMEM((hours, n_bld, rank // 2, 2 * i_share), bf16),
            pltpu.VMEM((rank // 2, 2 * i_share), bf16),
            pltpu.VMEM((n_bld, rank // 2, 2 * i_share), bf16),
            pltpu.VMEM((rank // 2, 2 * rank), f32),
            pltpu.VMEM((n_smp, rank // 2, 2 * rank), f32),
            pltpu.VMEM((n_smp, rank, j_share), bf16),
            pltpu.VMEM((n_smp, rank, j_share), bf16),
            pltpu.VMEM((rank, j_share), bf16),
            pltpu.VMEM((n_smp, rank, j_share), bf16),
            pltpu.VMEM((rank // 2, 2 * rank), f32),
            pltpu.VMEM((n_bld, rank // 2, 2 * rank), f32),
            pltpu.VMEM((pad, 2 * rank), f32),
            pltpu.VMEM((n_bld, pad, 2 * rank), f32),
            pltpu.VMEM((pad, 2 * rank), f32),
            pltpu.VMEM((n_smp, pad, 2 * rank), f32),
            pltpu.SemaphoreType.DMA((hours,)),
            pltpu.SemaphoreType.DMA((COUNT,)),
            pltpu.SemaphoreType.DMA((COUNT,)),
        ],
        compiler_params=pltpu.CompilerParams(
            collective_id=0, has_side_effects=True, vmem_limit_bytes=40 * 1024 * 1024
        ),
        name="als_sweeps",
    )(tensor, building_factor, hour_weights)


def solution(mesh):
    in_specs = (P(None, "smp", "bld"), P(None, "bld"), P())
    out_specs = (P(None, ("smp", "bld")), P(None, ("bld", "smp")), P())
    return jax.shard_map(local, mesh=mesh, in_specs=in_specs, out_specs=out_specs, check_vma=False)
```

time: 186 us -> 170 us (0.914)
  Pallas kernels: 178 us -> 162 us
    pallas_call x1, Pallas kernels: 178 us -> 162 us  [local(): pl.pallas_call(body, out_shape=(jax.ShapeDtypeStruct((rank, i_share), f32...]
where the time goes in v2:
time: 170 us
  Pallas kernels  162 us (95%)
  local copies, waits for them, and re-layouts  6.81 us (4%)
    pallas_call x1, Pallas kernels, local(): pl.pallas_call(body, out_shape=(jax.ShapeDtypeStruct((rank, i_share), f32...  162 us
    unnamed x9, local copies, waits for them, and re-layouts  6.81 us

profile of v2, /device:TPU:1, one launch (start us, length us, event | category | flops | bytes accessed | tf_op | source)
XLA Modules:
  0.0 169.6 jit_solution(8324700408160102918)
XLA Ops:
  0.6 0.0 copy-start
  0.6 3.4 %copy-done = bf16[4,1024,1024]{2,1,0:T(8,128)(2,1)S(1)} copy-done((bf16[4,1024,1024]{2,1,0:T(8,128)(2,1)S(1)}, bf16[4,1024,1024]{2,1,0:T(8,128)(2,1)}, u32[]{:S(2)}) %copy-start) | copy-done | bytes 8388632
  4.0 0.0 copy-start.1
  4.0 0.9 copy-done.1
  5.0 0.0 copy-start.2
  5.0 0.7 copy-done.2
  5.6 162.1 %als_sweeps.1 = (f32[64,64]{1,0:T(8,128)S(1)}, f32[64,128]{1,0:T(8,128)S(1)}, f32[4,64]{1,0:T(4,128)S(1)}) custom-call(bf16[4,1024,1024]{2,1,0:T(8,128)(2,1)S(1)} %copy-done, f32[64,1024]{1,0:T(8,128)S(1)} %copy-done.1, f32[4,64]{1,0:T(4,128)S(1)} %copy-done.2), custom_call_target="tpu_custom_call" | custom-call | tf_op jit(solution)/shard_map/als_sweeps/pallas_call | solution.py:356
  167.7 0.6 copy.9
  168.4 0.6 copy.10
  169.0 0.6 copy.11
Async XLA Ops:
  0.6 3.4 %copy-start = (bf16[4,1024,1024]{2,1,0:T(8,128)(2,1)S(1)}, bf16[4,1024,1024]{2,1,0:T(8,128)(2,1)}, u32[]{:S(2)}) copy-start(bf16[4,1024,1024]{2,1,0:T(8,128)(2,1)} %tensor_ref.1) | copy-start | bytes 25165828
  4.0 0.9 copy-start.1
  5.0 0.7 copy-start.2

commit v3 on v2

--- a/solution.py
+++ b/solution.py
@@ -41,15 +41,61 @@
     return jnp.concatenate([square[:half], square[half:]], axis=1)
 
 
-def unpack(packed):
-    half = packed.shape[1] // 2
-    return jnp.concatenate([packed[:, :half], packed[:, half:]], axis=0)
+def low_lanes(rows):
+    return lax.broadcasted_iota(jnp.int32, (rows, 128), 1) < 64
+
+
+def unpack_twice(packed):
+    turned = pltpu.roll(packed, 64, 1)
+    low = low_lanes(packed.shape[0])
+    return jnp.concatenate([jnp.where(low, packed, turned), jnp.where(low, turned, packed)], axis=0)
+
+
+def identity_twice(n):
+    rows = lax.broadcasted_iota(jnp.int32, (n, 2 * n), 0)
+    cols = lax.broadcasted_iota(jnp.int32, (n, 2 * n), 1)
+    return ((cols == rows) | (cols == rows + n)).astype(jnp.float32)
+
+
+def split(x):
+    high = x.astype(jnp.bfloat16).astype(jnp.float32)
+    rest = x - high
+    middle = rest.astype(jnp.bfloat16).astype(jnp.float32)
+    return high, middle, rest - middle
+
+
+def low16(*arrays):
+    return [array.astype(jnp.bfloat16) for array in arrays]
+
+
+def left_parts(a):
+    high, middle, rest = split(a)
+    low = low_lanes(a.shape[0])
+    one = jnp.concatenate(low16(high, jnp.where(low, middle, high)), axis=1)
+    two = jnp.where(low, rest, middle).astype(jnp.bfloat16)
+    return one, two
+
+
+def product(a, b):
+    one, two = left_parts(a)
+    high, middle, rest = low16(*split(b))
+    return dot16(one, jnp.concatenate([high, middle, high, rest], axis=0)) + dot16(
+        two, jnp.concatenate([high, middle], axis=0)
+    )
+
+
+def product_two_parts(a, b):
+    high, middle, _ = low16(*split(a))
+    over, under, _ = low16(*split(b))
+    return dot16(
+        jnp.concatenate([high, middle], axis=1), jnp.concatenate([over, under, over, under], axis=0)
+    )
 
 
 def regularized_inverse(gram):
     n = gram.shape[0]
-    eye = identity(n)
-    mean = jnp.sum(jnp.sum(gram * eye, axis=0, keepdims=True), axis=1, keepdims=True) / n
+    eye = identity_twice(n)
+    mean = jnp.sum(jnp.sum(gram * eye, axis=0, keepdims=True), axis=1, keepdims=True) / (2 * n)
     scale = 2.0 / ((n + 2 * RIDGE_SHARE) * mean)
     t = scale * (gram + RIDGE_SHARE * mean * eye)
     y = None
@@ -61,33 +107,24 @@
         factor = gain * (2.0 * eye - t)
         if step == 0:
             y = factor
-            t = dot32(t, factor)
+            t = product(t, factor)
         elif step < steps - 1:
-            both = dot32(jnp.concatenate([y, t], axis=0), factor)
+            both = product(jnp.concatenate([y, t], axis=0), factor)
             y, t = both[:n], both[n:]
         else:
-            y = dot32(y, factor)
+            y = product(y, factor)
     return scale * y
 
 
-def three_parts(x):
-    high = x.astype(jnp.bfloat16)
-    rest = x - high.astype(jnp.float32)
-    middle = rest.astype(jnp.bfloat16)
-    low = (rest - middle.astype(jnp.float32)).astype(jnp.bfloat16)
-    return jnp.concatenate([high, middle, low], axis=0)
-
-
 def scales_of(gram_raw, count):
-    eye = identity(gram_raw.shape[0])
-    diag_row = jnp.sum(gram_raw * eye, axis=0, keepdims=True)
-    diag_col = jnp.sum(gram_raw * eye, axis=1, keepdims=True)
-    inv_row = 1.0 / jnp.sqrt(diag_row / count + EPSILON)
-    inv_col = 1.0 / jnp.sqrt(diag_col / count + EPSILON)
+    n = gram_raw.shape[0]
+    diagonal = gram_raw * identity_twice(n)
+    inv_row = 1.0 / jnp.sqrt(jnp.sum(diagonal, axis=0, keepdims=True) / count + EPSILON)
+    inv_col = 1.0 / jnp.sqrt(jnp.sum(diagonal, axis=1, keepdims=True) / (2 * count) + EPSILON)
     return inv_row, inv_col
 
 
-RS1, AG1, GS, RS2, AG2, GB, P1, P2, COUNT = 0, 4, 8, 9, 10, 11, 12, 13, 14
+RS1, AG1, GS, RS2, AG2, GB, P1, P2, GB0, COUNT = 0, 4, 8, 9, 10, 11, 12, 13, 14, 15
 
 
 def kernel(
@@ -95,9 +132,9 @@
     tensor_ref, build_ref, hour_ref,
     sample_out, build_out, hour_out,
     slab, mixed, factor, s_slice, ub_slice,
-    gram_build, gram_sample, inv_sample, hour_rows, hour_cols, inv_b_col, inv_s_row, inv_s_col,
+    gram_build, gram_sample, inv_sample, inv_hour, hour_rhs, hour_cols, inv_b_col, inv_s_row, inv_s_col,
     rs1_send, rs1_recv, ag1_send, ag1_recv, gs_send, gs_recv,
-    rs2_send, rs2_recv, ag2_send, ag2_recv, gb_send, gb_recv, p1_send, p1_recv, p2_send, p2_recv,
+    rs2_send, rs2_recv, ag2_send, ag2_recv, gb_send, gb_recv, gb0_send, gb0_recv, p1_send, p1_recv, p2_send, p2_recv,
     load_sem, send_sems, recv_sems,
 ):
     hours, n_i, n_j = slab.shape
@@ -159,8 +196,7 @@
     for k in range(hours):
         load(k).start()
 
-    lane = lax.broadcasted_iota(jnp.int32, (half, 128), 1)
-    low_lane = lane < 64
+    low_lane = low_lanes(half)
     tile = 512
 
     def project(k):
@@ -174,38 +210,49 @@
         rs1_recv[k, bld] = rs1_send[k, bld]
         start_exchange("bld", lambda peer: rs1_send.at[k, peer], rs1_recv.at[k, bld], lambda step: RS1 + k)
 
-    def build_gram_start(gram):
+    def build_gram_start(gram, send, recv, sem):
         message = pack(gram)
-        gb_send[...] = message
-        gb_recv[bld] = message
-        start_exchange("bld", lambda peer: gb_send, gb_recv.at[bld], lambda step: GB)
-
-    def build_gram_finish():
-        finish_exchange(GB, gb_recv.at[pl.ds(0, n_bld - 1)])
-        total = gb_recv[0]
+        send[...] = message
+        recv[bld] = message
+        start_exchange("bld", lambda peer: send, recv.at[bld], lambda step: sem)
+
+    def build_gram_finish(recv, sem):
+        finish_exchange(sem, recv.at[pl.ds(0, n_bld - 1)])
+        total = recv[0]
         for b in range(1, n_bld):
-            total = total + gb_recv[b]
-        return unpack(total)
-
-    pad = hour_rows.shape[0]
-    rows_k = lax.broadcasted_iota(jnp.int32, (pad, hours * 128), 0)
-    lanes_k = lax.broadcasted_iota(jnp.int32, (pad, hours * 128), 1)
-    pick = (rows_k == lanes_k // 128).astype(jnp.float32)
-
-    hour_rows[...] = jnp.zeros_like(hour_rows)
-    hour_rows[0:hours, :] = hour_ref[...] / scale_up
-    hour_cols[...] = dot32(identity(rank), hour_rows[...], NT)
+            total = total + recv[b]
+        return unpack_twice(total)
+
+    pad = hour_rhs.shape[0]
+    pick_rows = lax.broadcasted_iota(jnp.int32, (pad, 128), 0)
+    quarter = lax.broadcasted_iota(jnp.int32, (pad, 128), 1) // 32
+    held = jnp.where(quarter == 0, 2, jnp.where(quarter == 1, 0, jnp.where(quarter == 2, 3, 1)))
+    pick = (pick_rows == held).astype(jnp.bfloat16)
+
+    def lane_sums(sums):
+        low = low_lanes(rank)
+        folded = [x + pltpu.roll(x, 64, 1) for x in sums]
+        first = jnp.where(low, folded[0], folded[1])
+        second = jnp.where(low, folded[2], folded[3])
+        first = first + pltpu.roll(first, 32, 1)
+        second = second + pltpu.roll(second, 96, 1)
+        upper = (lax.broadcasted_iota(jnp.int32, (rank, 128), 1) // 32) % 2 == 1
+        parts = low16(*split(jnp.where(upper, first, second)))
+        rows = dot16(jnp.concatenate([pick] * 3, axis=1), jnp.concatenate(parts, axis=1), NT)
+        return jnp.concatenate([rows, rows], axis=1)
+
+    hour_rhs[...] = jnp.zeros_like(hour_rhs)
+    hour_rhs[0:hours, 0:rank] = hour_ref[...] / scale_up
+    inv_hour[...] = identity_twice(rank)
+    hour_cols[...] = dot32(identity(rank), hour_rhs[:, 0:rank], NT)
     inv_b_col[...] = jnp.ones_like(inv_b_col)
-    start_factor = build_ref[...]
-    factor[...] = start_factor.astype(jnp.bfloat16)
-    gram0 = dot32(start_factor, start_factor, NT)
+    factor[...] = build_ref[...].astype(jnp.bfloat16)
 
     pl.semaphore_wait(barrier, n_bld + n_smp - 2)
-    build_gram_start(gram0)
     for k in range(hours):
         load(k).wait()
         project(k)
-    gram_build[...] = build_gram_finish()
+    build_gram_start(dot32(build_ref[...], build_ref[...], NT), gb0_send, gb0_recv, GB0)
 
     @pl.loop(0, SWEEPS)
     def _(sweep):
@@ -229,34 +276,40 @@
         ag1_recv[bld] = message
         start_exchange("bld", lambda peer: ag1_send, ag1_recv.at[bld], lambda step: AG1 + step[0])
 
-        gram_hour = dot32(hour_cols[...], hour_rows[...])
+        @pl.when(sweep == 0)
+        def _():
+            gram_build[...] = build_gram_finish(gb0_recv, GB0)
+
+        gram_hour = dot32(hour_cols[...], dot32(hour_rhs[:, 0:rank], inv_hour[...]))
         inverse = regularized_inverse(gram_build[...] * gram_hour)
         inv_sample[...] = inverse
-        parts = three_parts(inverse)
+        parts = jnp.concatenate(low16(*split(inverse)), axis=0)[:, :rank]
+        gram_part = jnp.zeros((rank, rank), jnp.float32)
 
         for order, dy in enumerate((0, 1, 3, 2)):
             chunk = (y - dy + 4) % 4
             first = chunk * 4
             finish_exchange(AG1 + dy, ag1_recv.at[pl.ds(0, 3 if dy == 0 else 4)])
+            columns = []
             for m in range(2):
                 even = ag1_recv[first + 2 * m].astype(jnp.float32)
                 odd = ag1_recv[first + 2 * m + 1].astype(jnp.float32)
                 top = jnp.where(low_lane, even, pltpu.roll(odd, 64, 1))
                 low = jnp.where(low_lane, pltpu.roll(even, 64, 1), odd)
-                columns = jnp.concatenate([top, low], axis=0).astype(jnp.bfloat16)
-                solved = dot16(parts, columns)
-                solved = solved[:rank] + (solved[rank : 2 * rank] + solved[2 * rank :])
-                where = pl.multiple_of(chunk * 256 + m * 128, 128)
-                factor[:, pl.ds(where, 128)] = solved.astype(jnp.bfloat16)
+                columns.append(jnp.concatenate([top, low], axis=0).astype(jnp.bfloat16))
+            solved = dot16(parts, jnp.concatenate(columns, axis=1))
+            solved = solved[:rank] + (solved[rank : 2 * rank] + solved[2 * rank :])
+            solved = solved.astype(jnp.bfloat16)
             rows = pl.ds(pl.multiple_of(chunk * 256, 256), 256)
+            gram_part = gram_part + dot16(solved, solved, NT)
             if order == 3:
-                gram_part = pack(dot16(factor[...], factor[...], NT))
-                gs_send[...] = gram_part
-                gs_recv[smp] = gram_part
+                message = pack(gram_part)
+                gs_send[...] = message
+                gs_recv[smp] = message
                 start_exchange("smp", lambda peer: gs_send, gs_recv.at[smp], lambda step: GS)
             for k in range(hours):
                 for j in range(0, n_j, tile):
-                    block = dot16(factor[:, rows], slab[k, rows, j : j + tile])
+                    block = dot16(solved, slab[k, rows, j : j + tile])
                     if order == 0:
                         mixed[k, :, j : j + tile] = block
                     else:
@@ -275,7 +328,7 @@
         gram_raw = gs_recv[0]
         for s in range(1, n_smp):
             gram_raw = gram_raw + gs_recv[s]
-        gram_raw = unpack(gram_raw)
+        gram_raw = unpack_twice(gram_raw)
         inv_row, inv_col = scales_of(gram_raw, samples_total)
         inv_s_row[...] = jnp.broadcast_to(inv_row, inv_s_row.shape)
         inv_s_col[...] = jnp.broadcast_to(inv_col, inv_s_col.shape)
@@ -286,7 +339,7 @@
         total = rs2_recv[0].astype(jnp.float32)
         for s in range(1, n_smp):
             total = total + rs2_recv[s].astype(jnp.float32)
-        unscaled = dot32(inverse, total)
+        unscaled = product_two_parts(inverse, total)
         ub_slice[...] = unscaled
         message = unscaled.astype(jnp.bfloat16)
         ag2_send[...] = message
@@ -300,14 +353,13 @@
             for s in range(n_smp):
                 acc = acc + mixed[k, :, s * 128 : (s + 1) * 128] * ag2_recv[s].astype(jnp.float32)
             sums.append(acc)
-        hour_terms = dot32(pick, jnp.concatenate(sums, axis=1), NT)
-        message = jnp.concatenate([hour_terms, jnp.zeros_like(hour_terms)], axis=1)
+        message = lane_sums(sums)
         p1_send[...] = message
         p1_recv[bld] = message
         start_exchange("bld", lambda peer: p1_send, p1_recv.at[bld], lambda step: P1)
         for s in range(n_smp):
             factor[:, s * 128 : (s + 1) * 128] = ag2_recv[s]
-        build_gram_start(dot16(factor[...], factor[...], NT))
+        build_gram_start(dot16(factor[...], factor[...], NT), gb_send, gb_recv, GB)
 
         @pl.when(sweep < SWEEPS - 1)
         def _():
@@ -322,23 +374,30 @@
         p2_recv[smp] = total
         start_exchange("smp", lambda peer: p2_send, p2_recv.at[smp], lambda step: P2)
 
-        gram_raw = build_gram_finish()
+        gram_raw = build_gram_finish(gb_recv, GB)
         inv_row, inv_col = scales_of(gram_raw, buildings_total)
         inv_b_col[...] = jnp.broadcast_to(inv_col, inv_b_col.shape)
         gram_build[...] = gram_raw * (inv_col * inv_row)
         inverse = regularized_inverse(gram_sample[...] * gram_build[...])
+        inv_hour[...] = inverse
+        one, two = left_parts(inverse)
+        scale_row = inv_row * inv_s_row[0:1, :]
 
         finish_exchange(P2, p2_recv.at[pl.ds(0, n_smp - 1)])
-        hour_sum = p2_recv[0]
+        total = p2_recv[0]
         for s in range(1, n_smp):
-            hour_sum = hour_sum + p2_recv[s]
-        hour_rhs = hour_sum[:, :rank] * (inv_row * inv_s_row[0:1, :])
-        hour_cols[...] = dot32(inverse, hour_rhs, NT)
-        hour_rows[...] = dot32(hour_rhs, inverse)
-
-    sample_out[...] = dot32(inv_sample[...], unpack(s_slice[...])) * inv_s_col[:, 0:1]
+            total = total + p2_recv[s]
+        right = total * scale_row
+        hour_rhs[...] = right
+        high, middle, rest = split(right)
+        low = low_lanes(pad)
+        both = jnp.where(low, high, middle).astype(jnp.bfloat16)
+        far = jnp.where(low, high, rest).astype(jnp.bfloat16)
+        hour_cols[...] = dot16(one, jnp.concatenate([both, far], axis=1), NT) + dot16(two, both, NT)
+
+    sample_out[...] = product(inv_sample[...], unpack_twice(s_slice[...]))[:, :rank] * inv_s_col[:, 0:1]
     build_out[...] = ub_slice[...] * inv_b_col[:, 0:1]
-    hour_out[...] = hour_rows[0:hours, :] * scale_up
+    hour_out[...] = dot32(hour_rhs[:, 0:rank], inv_hour[:, 0:rank])[0:hours] * scale_up
 
 
 def local(tensor, building_factor, hour_weights):
@@ -368,13 +427,14 @@
             pltpu.VMEM((rank, n_j), bf16),
             pltpu.VMEM((rank // 2, 2 * i_share), f32),
             pltpu.VMEM((rank, j_share), f32),
-            pltpu.VMEM((rank, rank), f32),
-            pltpu.VMEM((rank, rank), f32),
-            pltpu.VMEM((rank, rank), f32),
-            pltpu.VMEM((pad, rank), f32),
+            pltpu.VMEM((rank, 2 * rank), f32),
+            pltpu.VMEM((rank, 2 * rank), f32),
+            pltpu.VMEM((rank, 2 * rank), f32),
+            pltpu.VMEM((rank, 2 * rank), f32),
+            pltpu.VMEM((pad, 2 * rank), f32),
             pltpu.VMEM((rank, pad), f32),
             pltpu.VMEM((rank, pad), f32),
-            pltpu.VMEM((pad, rank), f32),
+            pltpu.VMEM((pad, 2 * rank), f32),
             pltpu.VMEM((rank, pad), f32),
             pltpu.VMEM((hours, n_bld, rank // 2, 2 * i_share), bf16),
             pltpu.VMEM((hours, n_bld, rank // 2, 2 * i_share), bf16),
@@ -388,6 +448,8 @@
             pltpu.VMEM((n_smp, rank, j_share), bf16),
             pltpu.VMEM((rank // 2, 2 * rank), f32),
             pltpu.VMEM((n_bld, rank // 2, 2 * rank), f32),
+            pltpu.VMEM((rank // 2, 2 * rank), f32),
+            pltpu.VMEM((n_bld, rank // 2, 2 * rank), f32),
             pltpu.VMEM((pad, 2 * rank), f32),
             pltpu.VMEM((n_bld, pad, 2 * rank), f32),
             pltpu.VMEM((pad, 2 * rank), f32),
@@ -397,7 +459,7 @@
             pltpu.SemaphoreType.DMA((COUNT,)),
         ],
         compiler_params=pltpu.CompilerParams(
-            collective_id=0, has_side_effects=True, vmem_limit_bytes=40 * 1024 * 1024
+            collective_id=0, has_side_effects=True, vmem_limit_bytes=60 * 1024 * 1024
         ),
         name="als_sweeps",
     )(tensor, building_factor, hour_weights)

time: 170 us -> 164 us (0.965)
  Pallas kernels: 162 us -> 159 us
  local copies, waits for them, and re-layouts: 6.81 us -> 3.99 us
    pallas_call x1, Pallas kernels: 162 us -> 159 us  [local(): pl.pallas_call(body, out_shape=(jax.ShapeDtypeStruct((rank, i_share), f32...]
    unnamed x9 -> x3, local copies, waits for them, and re-layouts: 6.81 us -> 3.99 us
where the time goes in v3:
time: 164 us
  Pallas kernels  159 us (97%)
  local copies, waits for them, and re-layouts  3.99 us (2%)
    pallas_call x1, Pallas kernels, local(): pl.pallas_call(body, out_shape=(jax.ShapeDtypeStruct((rank, i_share), f32...  159 us
    unnamed x3, local copies, waits for them, and re-layouts  3.99 us

profile of v3, /device:TPU:1, one launch (start us, length us, event | category | flops | bytes accessed | tf_op | source)
XLA Modules:
  0.0 163.7 jit_solution(17782187843965485829)
XLA Ops:
  0.6 159.1 %als_sweeps.1 = (f32[64,64]{1,0:T(8,128)}, f32[64,128]{1,0:T(8,128)}, f32[4,64]{1,0:T(4,128)}) custom-call(bf16[4,1024,1024]{2,1,0:T(8,128)(2,1)} %tensor_ref.1, f32[64,1024]{1,0:T(8,128)} %build_ref.1, f32[4,64]{1,0:T(4,128)} %hour_ref.1), custom_call_target="tpu_custom_call" | custom-call | tf_op jit(solution)/shard_map/als_sweeps/pallas_call | solution.py:415
  159.7 1.4 copy.9
  161.1 1.4 copy.10
  162.4 1.2 copy.11

commit v4 on v3

--- a/solution.py
+++ b/solution.py
@@ -124,14 +124,14 @@
     return inv_row, inv_col
 
 
-RS1, AG1, GS, RS2, AG2, GB, P1, P2, GB0, COUNT = 0, 4, 8, 9, 10, 11, 12, 13, 14, 15
+RS1, AG1, AG2, PAIR, GS, RS2, GB, P1, P2, GB0, GP, COUNT = 0, 4, 8, 12, 16, 17, 18, 19, 20, 21, 22, 23
 
 
 def kernel(
     n_smp, n_bld, samples_total, buildings_total,
     tensor_ref, build_ref, hour_ref,
     sample_out, build_out, hour_out,
-    slab, mixed, factor, s_slice, ub_slice,
+    slab, mixed, partial, own, pair_send, pair_recv, gp_send, gp_recv, s_slice, ub_slice,
     gram_build, gram_sample, inv_sample, inv_hour, hour_rhs, hour_cols, inv_b_col, inv_s_row, inv_s_col,
     rs1_send, rs1_recv, ag1_send, ag1_recv, gs_send, gs_recv,
     rs2_send, rs2_recv, ag2_send, ag2_recv, gb_send, gb_recv, gb0_send, gb0_recv, p1_send, p1_recv, p2_send, p2_recv,
@@ -158,10 +158,22 @@
         return ((x_lo + dx) % 2) * 4 + (z + dz) % 4
 
     bld_peers = [bld_peer(step) for step in BLD_STEPS]
+    like_steps = [step for step in BLD_STEPS if step[2] == 0]
+    like_peers = [bld_peer(step) for step in like_steps]
+    partner = bld_peer((0, 0, 1))
+    chip = bld // 2
+    n_chip = n_bld // 2
     smp_peers = [smp_peer(step) for step in SMP_STEPS]
 
     def start_exchange(axis, piece_of, place, sem_of):
-        peers, steps = (bld_peers, BLD_STEPS) if axis == "bld" else (smp_peers, SMP_STEPS)
+        if axis == "like":
+            peers, steps, axis = like_peers, like_steps, "bld"
+        elif axis == "partner":
+            peers, steps, axis = [partner], [(0, 0, 1)], "bld"
+        elif axis == "bld":
+            peers, steps = bld_peers, BLD_STEPS
+        else:
+            peers, steps = smp_peers, SMP_STEPS
         for peer, step in zip(peers, steps):
             pltpu.make_async_remote_copy(
                 src_ref=piece_of(peer),
@@ -199,16 +211,40 @@
     low_lane = low_lanes(half)
     tile = 512
 
-    def project(k):
-        for i in range(0, n_i, tile):
-            block = dot16(factor[...], slab[k, i : i + tile, :], NT)
-            for m in range(tile // 128):
-                top, low = block[:half, m * 128 : (m + 1) * 128], block[half:, m * 128 : (m + 1) * 128]
-                b = 2 * (i // 128 + m)
-                rs1_send[k, b] = jnp.where(low_lane, top, pltpu.roll(low, 64, 1)).astype(rs1_send.dtype)
-                rs1_send[k, b + 1] = jnp.where(low_lane, pltpu.roll(top, 64, 1), low).astype(rs1_send.dtype)
-        rs1_recv[k, bld] = rs1_send[k, bld]
-        start_exchange("bld", lambda peer: rs1_send.at[k, peer], rs1_recv.at[k, bld], lambda step: RS1 + k)
+    def scatter(k, i, block):
+        for m in range(tile // 128):
+            top, low = block[:half, m * 128 : (m + 1) * 128], block[half:, m * 128 : (m + 1) * 128]
+            moved = pltpu.roll(jnp.where(low_lane, low, top), 64, 1)
+            even = jnp.where(low_lane, top, moved)
+            odd = jnp.where(low_lane, moved, low)
+            own[k, i // 128 + m] = jnp.where(core == 0, even, odd)
+            pair_send[k, i // 128 + m] = jnp.where(core == 0, odd, even).astype(pair_send.dtype)
+
+    def pair_start(k):
+        start_exchange("partner", lambda peer: pair_send.at[k], pair_recv.at[k], lambda step: PAIR + k)
+
+    def pair_finish(k):
+        finish_exchange(PAIR + k, pair_recv.at[k])
+        for c in range(n_chip):
+            rs1_send[k, c] = (own[k, c] + pair_recv[k, c].astype(jnp.float32)).astype(rs1_send.dtype)
+        rs1_recv[k, chip] = rs1_send[k, chip]
+        start_exchange("like", lambda peer: rs1_send.at[k, peer // 2], rs1_recv.at[k, chip], lambda step: RS1 + k)
+
+    def slices(ref, index, groups):
+        parts = []
+        for group in groups:
+            for first in (0, 4):
+                parts.append(ref[index + (pl.ds(pl.multiple_of((first + group) * 128, 128), 128),)])
+        return jnp.concatenate(parts, axis=-1)
+
+    def gathered(groups):
+        parts = []
+        for group in groups:
+            parts += [ag2_recv[group], ag2_recv[4 + group]]
+        return jnp.concatenate(parts, axis=1)
+
+    def project(k, i, groups):
+        return dot16(gathered(groups), slices(slab, (k, slice(i, i + tile)), groups), NT)
 
     def build_gram_start(gram, send, recv, sem):
         message = pack(gram)
@@ -217,9 +253,10 @@
         start_exchange("bld", lambda peer: send, recv.at[bld], lambda step: sem)
 
     def build_gram_finish(recv, sem):
-        finish_exchange(sem, recv.at[pl.ds(0, n_bld - 1)])
+        others = recv.shape[0] - 1
+        finish_exchange(sem, recv.at[pl.ds(0, others)])
         total = recv[0]
-        for b in range(1, n_bld):
+        for b in range(1, others + 1):
             total = total + recv[b]
         return unpack_twice(total)
 
@@ -246,18 +283,24 @@
     inv_hour[...] = identity_twice(rank)
     hour_cols[...] = dot32(identity(rank), hour_rhs[:, 0:rank], NT)
     inv_b_col[...] = jnp.ones_like(inv_b_col)
-    factor[...] = build_ref[...].astype(jnp.bfloat16)
-
-    pl.semaphore_wait(barrier, n_bld + n_smp - 2)
+    start_factor = build_ref[...].astype(jnp.bfloat16)
     for k in range(hours):
         load(k).wait()
-        project(k)
+        for i in range(0, n_i, tile):
+            scatter(k, i, dot16(start_factor, slab[k, i : i + tile, :], NT))
+        if k == 1:
+            pl.semaphore_wait(barrier, n_bld + n_smp - 2)
+            pair_start(0)
+        if k >= 1:
+            pair_start(k)
+            pair_finish(k - 1)
+    pair_finish(hours - 1)
     build_gram_start(dot32(build_ref[...], build_ref[...], NT), gb0_send, gb0_recv, GB0)
 
     @pl.loop(0, SWEEPS)
     def _(sweep):
         for k in range(hours):
-            finish_exchange(RS1 + k, rs1_recv.at[k, pl.ds(0, n_bld - 1)])
+            finish_exchange(RS1 + k, rs1_recv.at[k, pl.ds(0, n_chip - 1)])
         right = None
         for k in range(hours):
             col = hour_cols[:, k : k + 1] * inv_b_col[:, 0:1]
@@ -267,8 +310,8 @@
                 jnp.broadcast_to(col[half:], (half, 128)),
             )
             total = rs1_recv[k, 0].astype(jnp.float32)
-            for b in range(1, n_bld):
-                total = total + rs1_recv[k, b].astype(jnp.float32)
+            for c in range(1, n_chip):
+                total = total + rs1_recv[k, c].astype(jnp.float32)
             right = both * total if right is None else right + both * total
         s_slice[...] = right
         message = right.astype(jnp.bfloat16)
@@ -294,8 +337,9 @@
             for m in range(2):
                 even = ag1_recv[first + 2 * m].astype(jnp.float32)
                 odd = ag1_recv[first + 2 * m + 1].astype(jnp.float32)
-                top = jnp.where(low_lane, even, pltpu.roll(odd, 64, 1))
-                low = jnp.where(low_lane, pltpu.roll(even, 64, 1), odd)
+                moved = pltpu.roll(jnp.where(low_lane, odd, even), 64, 1)
+                top = jnp.where(low_lane, even, moved)
+                low = jnp.where(low_lane, moved, odd)
                 columns.append(jnp.concatenate([top, low], axis=0).astype(jnp.bfloat16))
             solved = dot16(parts, jnp.concatenate(columns, axis=1))
             solved = solved[:rank] + (solved[rank : 2 * rank] + solved[2 * rank :])
@@ -344,27 +388,65 @@
         message = unscaled.astype(jnp.bfloat16)
         ag2_send[...] = message
         ag2_recv[smp] = message
-        start_exchange("smp", lambda peer: ag2_send, ag2_recv.at[smp], lambda step: AG2)
-        finish_exchange(AG2, ag2_recv.at[pl.ds(0, n_smp - 1)])
-
-        sums = []
-        for k in range(hours):
-            acc = jnp.zeros((rank, 128), jnp.float32)
-            for s in range(n_smp):
-                acc = acc + mixed[k, :, s * 128 : (s + 1) * 128] * ag2_recv[s].astype(jnp.float32)
-            sums.append(acc)
+        start_exchange("smp", lambda peer: ag2_send, ag2_recv.at[smp], lambda step: AG2 + step[1])
+
+        sums = [jnp.zeros((rank, 128), jnp.float32) for _ in range(hours)]
+        gram_part = jnp.zeros((rank, rank), jnp.float32)
+        before_last = sweep < SWEEPS - 1
+        groups = [(z - dz + 4) % 4 for dz in (0, 1, 3, 2)]
+        early = {k: groups[:2] if k < 2 else groups[:1] for k in range(hours)}
+        for order, dz in enumerate((0, 1, 3, 2)):
+            finish_exchange(AG2 + dz, ag2_recv.at[pl.ds(0, 1 if dz == 0 else 2)])
+            group = groups[order]
+            solved = gathered([group])
+            gram_part = gram_part + dot16(solved, solved, NT)
+            wide = solved.astype(jnp.float32)
+            for k in range(hours):
+                terms = slices(mixed, (k, slice(None)), [group]) * wide
+                sums[k] = sums[k] + (terms[:, :128] + terms[:, 128:])
+            if order < 2:
+
+                @pl.when(before_last)
+                def _():
+                    for k in range(hours):
+                        if order < len(early[k]):
+                            for i in range(0, n_i, tile):
+                                block = project(k, i, [group])
+                                if order == 0:
+                                    partial[k, :, i : i + tile] = block
+                                else:
+                                    partial[k, :, i : i + tile] += block
+
         message = lane_sums(sums)
         p1_send[...] = message
         p1_recv[bld] = message
         start_exchange("bld", lambda peer: p1_send, p1_recv.at[bld], lambda step: P1)
-        for s in range(n_smp):
-            factor[:, s * 128 : (s + 1) * 128] = ag2_recv[s]
-        build_gram_start(dot16(factor[...], factor[...], NT), gb_send, gb_recv, GB)
-
-        @pl.when(sweep < SWEEPS - 1)
+        message = pack(gram_part)
+        gp_send[...] = message
+        start_exchange("partner", lambda peer: gp_send, gp_recv, lambda step: GP)
+
+        def finish_project(k):
+            left = groups[len(early[k]) :]
+            for i in range(0, n_i, tile):
+                scatter(k, i, partial[k, :, i : i + tile] + project(k, i, left))
+            pair_start(k)
+
+        @pl.when(before_last)
         def _():
-            for k in range(hours):
-                project(k)
+            finish_project(0)
+
+        finish_exchange(GP, gp_recv)
+        message = gp_send[...] + gp_recv[...]
+        gb_send[...] = message
+        gb_recv[chip] = message
+        start_exchange("like", lambda peer: gb_send, gb_recv.at[chip], lambda step: GB)
+
+        @pl.when(before_last)
+        def _():
+            for k in range(1, hours):
+                finish_project(k)
+                pair_finish(k - 1)
+            pair_finish(hours - 1)
 
         finish_exchange(P1, p1_recv.at[pl.ds(0, n_bld - 1)])
         total = p1_recv[0]
@@ -398,6 +480,15 @@
     sample_out[...] = product(inv_sample[...], unpack_twice(s_slice[...]))[:, :rank] * inv_s_col[:, 0:1]
     build_out[...] = ub_slice[...] * inv_b_col[:, 0:1]
     hour_out[...] = dot32(hour_rhs[:, 0:rank], inv_hour[:, 0:rank])[0:hours] * scale_up
+
+
+def put_out(a_ref, b_ref, c_ref, a_out, b_out, c_out, sems):
+    pairs = ((a_ref, a_out), (b_ref, b_out), (c_ref, c_out))
+    copies = [pltpu.make_async_copy(x, y, sems.at[n]) for n, (x, y) in enumerate(pairs)]
+    for copy in copies:
+        copy.start()
+    for copy in copies:
+        copy.wait()
 
 
 def local(tensor, building_factor, hour_weights):
@@ -412,7 +503,7 @@
     body = functools.partial(kernel, n_smp, n_bld, n_i * n_smp, n_j * n_bld)
     vmem = pl.BlockSpec(memory_space=pltpu.VMEM)
     pad = 8
-    return pl.pallas_call(
+    results = pl.pallas_call(
         body,
         out_shape=(
             jax.ShapeDtypeStruct((rank, i_share), f32),
@@ -424,7 +515,12 @@
         scratch_shapes=[
             pltpu.VMEM((hours, n_i, n_j), bf16),
             pltpu.VMEM((hours, rank, n_j), f32),
-            pltpu.VMEM((rank, n_j), bf16),
+            pltpu.VMEM((hours, rank, n_i), f32),
+            pltpu.VMEM((hours, n_bld // 2, rank // 2, 2 * i_share), f32),
+            pltpu.VMEM((hours, n_bld // 2, rank // 2, 2 * i_share), bf16),
+            pltpu.VMEM((hours, n_bld // 2, rank // 2, 2 * i_share), bf16),
+            pltpu.VMEM((rank // 2, 2 * rank), f32),
+            pltpu.VMEM((rank // 2, 2 * rank), f32),
             pltpu.VMEM((rank // 2, 2 * i_share), f32),
             pltpu.VMEM((rank, j_share), f32),
             pltpu.VMEM((rank, 2 * rank), f32),
@@ -436,8 +532,8 @@
             pltpu.VMEM((rank, pad), f32),
             pltpu.VMEM((pad, 2 * rank), f32),
             pltpu.VMEM((rank, pad), f32),
-            pltpu.VMEM((hours, n_bld, rank // 2, 2 * i_share), bf16),
-            pltpu.VMEM((hours, n_bld, rank // 2, 2 * i_share), bf16),
+            pltpu.VMEM((hours, n_bld // 2, rank // 2, 2 * i_share), bf16),
+            pltpu.VMEM((hours, n_bld // 2, rank // 2, 2 * i_share), bf16),
             pltpu.VMEM((rank // 2, 2 * i_share), bf16),
             pltpu.VMEM((n_bld, rank // 2, 2 * i_share), bf16),
             pltpu.VMEM((rank // 2, 2 * rank), f32),
@@ -447,7 +543,7 @@
             pltpu.VMEM((rank, j_share), bf16),
             pltpu.VMEM((n_smp, rank, j_share), bf16),
             pltpu.VMEM((rank // 2, 2 * rank), f32),
-            pltpu.VMEM((n_bld, rank // 2, 2 * rank), f32),
+            pltpu.VMEM((n_bld // 2, rank // 2, 2 * rank), f32),
             pltpu.VMEM((rank // 2, 2 * rank), f32),
             pltpu.VMEM((n_bld, rank // 2, 2 * rank), f32),
             pltpu.VMEM((pad, 2 * rank), f32),
@@ -463,6 +559,14 @@
         ),
         name="als_sweeps",
     )(tensor, building_factor, hour_weights)
+    return pl.pallas_call(
+        put_out,
+        out_shape=tuple(jax.ShapeDtypeStruct(x.shape, x.dtype) for x in results),
+        in_specs=[vmem] * 3,
+        out_specs=(pl.BlockSpec(memory_space=pl.ANY),) * 3,
+        scratch_shapes=[pltpu.SemaphoreType.DMA((3,))],
+        name="put_out",
+    )(*results)
 
 
 def solution(mesh):

time: 164 us -> 157 us (0.957)
  local copies, waits for them, and re-layouts: 3.99 us -> 0 us
  Pallas kernels: 159 us -> 156 us
    pallas_call x1, Pallas kernels: 159 us -> 155 us  [local(): pl.pallas_call(body, out_shape=(jax.ShapeDtypeStruct((rank, i_share), f32...]
    unnamed x3 -> x0, local copies, waits for them, and re-layouts: 3.99 us -> none
where the time goes in v4:
time: 157 us
  Pallas kernels  156 us (99%)
    pallas_call x1, Pallas kernels, local(): pl.pallas_call(body, out_shape=(jax.ShapeDtypeStruct((rank, i_share), f32...  155 us

profile of v4, /device:TPU:1, one launch (start us, length us, event | category | flops | bytes accessed | tf_op | source)
XLA Modules:
  0.0 156.6 jit_solution(6931143093341677938)
XLA Ops:
  0.6 154.6 %als_sweeps.1 = (f32[64,64]{1,0:T(8,128)}, f32[64,128]{1,0:T(8,128)}, f32[4,64]{1,0:T(4,128)}) custom-call(bf16[4,1024,1024]{2,1,0:T(8,128)(2,1)} %tensor_ref.1, f32[64,1024]{1,0:T(8,128)} %build_ref.1, f32[4,64]{1,0:T(4,128)} %hour_ref.1), custom_call_target="tpu_custom_call" | custom-call | tf_op jit(solution)/shard_map/als_sweeps/pallas_call | solution.py:506
  155.2 1.4 put_out.1

commit v5 on v4

--- a/solution.py
+++ b/solution.py
@@ -81,14 +81,6 @@
     high, middle, rest = low16(*split(b))
     return dot16(one, jnp.concatenate([high, middle, high, rest], axis=0)) + dot16(
         two, jnp.concatenate([high, middle], axis=0)
-    )
-
-
-def product_two_parts(a, b):
-    high, middle, _ = low16(*split(a))
-    over, under, _ = low16(*split(b))
-    return dot16(
-        jnp.concatenate([high, middle], axis=1), jnp.concatenate([over, under, over, under], axis=0)
     )
 
 
@@ -131,8 +123,8 @@
     n_smp, n_bld, samples_total, buildings_total,
     tensor_ref, build_ref, hour_ref,
     sample_out, build_out, hour_out,
-    slab, mixed, partial, own, pair_send, pair_recv, gp_send, gp_recv, s_slice, ub_slice,
-    gram_build, gram_sample, inv_sample, inv_hour, hour_rhs, hour_cols, inv_b_col, inv_s_row, inv_s_col,
+    slab, mixed, partial, factor, own, pair_send, pair_recv, gp_send, gp_recv, s_slice, b_slice,
+    gram_build, gram_sample, inv_sample, inv_build, inv_hour, hour_rhs, hour_cols, inv_b_col, inv_s_row, inv_s_col,
     rs1_send, rs1_recv, ag1_send, ag1_recv, gs_send, gs_recv,
     rs2_send, rs2_recv, ag2_send, ag2_recv, gb_send, gb_recv, gb0_send, gb0_recv, p1_send, p1_recv, p2_send, p2_recv,
     load_sem, send_sems, recv_sems,
@@ -202,11 +194,17 @@
     for peer in smp_peers:
         pl.semaphore_signal(barrier, inc=1, device_id={"smp": peer}, device_id_type=MESH)
 
-    def load(k):
-        return pltpu.make_async_copy(tensor_ref.at[k], slab.at[k], load_sem.at[k])
+    def place(s):
+        return (s % 4) * 2 + s // 4
+
+    def load(k, s):
+        from_ref = tensor_ref.at[k, :, s * 128 : (s + 1) * 128]
+        to_ref = slab.at[k, :, place(s) * 128 : (place(s) + 1) * 128]
+        return pltpu.make_async_copy(from_ref, to_ref, load_sem.at[k, s])
 
     for k in range(hours):
-        load(k).start()
+        for s in range(n_smp):
+            load(k, s).start()
 
     low_lane = low_lanes(half)
     tile = 512
@@ -231,20 +229,19 @@
         start_exchange("like", lambda peer: rs1_send.at[k, peer // 2], rs1_recv.at[k, chip], lambda step: RS1 + k)
 
     def slices(ref, index, groups):
-        parts = []
-        for group in groups:
-            for first in (0, 4):
-                parts.append(ref[index + (pl.ds(pl.multiple_of((first + group) * 128, 128), 128),)])
-        return jnp.concatenate(parts, axis=-1)
-
-    def gathered(groups):
-        parts = []
-        for group in groups:
-            parts += [ag2_recv[group], ag2_recv[4 + group]]
-        return jnp.concatenate(parts, axis=1)
+        parts = [ref[index + (pl.ds(pl.multiple_of(group * 256, 256), 256),)] for group in groups]
+        return parts[0] if len(parts) == 1 else jnp.concatenate(parts, axis=-1)
+
+    def gathered(group):
+        return jnp.concatenate([ag2_recv[group], ag2_recv[4 + group]], axis=1)
+
+    def solve_columns(parts, columns):
+        solved = dot16(parts, columns)
+        solved = solved[:rank] + (solved[rank : 2 * rank] + solved[2 * rank :])
+        return solved.astype(jnp.bfloat16)
 
     def project(k, i, groups):
-        return dot16(gathered(groups), slices(slab, (k, slice(i, i + tile)), groups), NT)
+        return dot16(slices(factor, (slice(None),), groups), slices(slab, (k, slice(i, i + tile)), groups), NT)
 
     def build_gram_start(gram, send, recv, sem):
         message = pack(gram)
@@ -283,9 +280,13 @@
     inv_hour[...] = identity_twice(rank)
     hour_cols[...] = dot32(identity(rank), hour_rhs[:, 0:rank], NT)
     inv_b_col[...] = jnp.ones_like(inv_b_col)
-    start_factor = build_ref[...].astype(jnp.bfloat16)
+    order_of = sorted(range(n_smp), key=place)
+    start_factor = jnp.concatenate(
+        [build_ref[:, s * 128 : (s + 1) * 128] for s in order_of], axis=1
+    ).astype(jnp.bfloat16)
     for k in range(hours):
-        load(k).wait()
+        for s in range(n_smp):
+            load(k, s).wait()
         for i in range(0, n_i, tile):
             scatter(k, i, dot16(start_factor, slab[k, i : i + tile, :], NT))
         if k == 1:
@@ -329,31 +330,26 @@
         parts = jnp.concatenate(low16(*split(inverse)), axis=0)[:, :rank]
         gram_part = jnp.zeros((rank, rank), jnp.float32)
 
-        for order, dy in enumerate((0, 1, 3, 2)):
-            chunk = (y - dy + 4) % 4
-            first = chunk * 4
-            finish_exchange(AG1 + dy, ag1_recv.at[pl.ds(0, 3 if dy == 0 else 4)])
+        for order, steps in enumerate(((0,), (1, 3), (2,))):
+            chunks = [(y - dy + 4) % 4 for dy in steps]
             columns = []
-            for m in range(2):
-                even = ag1_recv[first + 2 * m].astype(jnp.float32)
-                odd = ag1_recv[first + 2 * m + 1].astype(jnp.float32)
-                moved = pltpu.roll(jnp.where(low_lane, odd, even), 64, 1)
-                top = jnp.where(low_lane, even, moved)
-                low = jnp.where(low_lane, moved, odd)
-                columns.append(jnp.concatenate([top, low], axis=0).astype(jnp.bfloat16))
-            solved = dot16(parts, jnp.concatenate(columns, axis=1))
-            solved = solved[:rank] + (solved[rank : 2 * rank] + solved[2 * rank :])
-            solved = solved.astype(jnp.bfloat16)
-            rows = pl.ds(pl.multiple_of(chunk * 256, 256), 256)
-            gram_part = gram_part + dot16(solved, solved, NT)
-            if order == 3:
-                message = pack(gram_part)
-                gs_send[...] = message
-                gs_recv[smp] = message
-                start_exchange("smp", lambda peer: gs_send, gs_recv.at[smp], lambda step: GS)
+            for dy, chunk in zip(steps, chunks):
+                finish_exchange(AG1 + dy, ag1_recv.at[pl.ds(0, 3 if dy == 0 else 4)])
+                for m in range(2):
+                    even = ag1_recv[chunk * 4 + 2 * m].astype(jnp.float32)
+                    odd = ag1_recv[chunk * 4 + 2 * m + 1].astype(jnp.float32)
+                    moved = pltpu.roll(jnp.where(low_lane, odd, even), 64, 1)
+                    top = jnp.where(low_lane, even, moved)
+                    low = jnp.where(low_lane, moved, odd)
+                    columns.append(jnp.concatenate([top, low], axis=0).astype(jnp.bfloat16))
+            solved = solve_columns(parts, jnp.concatenate(columns, axis=1))
+            rows = [pl.ds(pl.multiple_of(chunk * 256, 256), 256) for chunk in chunks]
+            if order < 2:
+                gram_part = gram_part + dot16(solved, solved, NT)
             for k in range(hours):
                 for j in range(0, n_j, tile):
-                    block = dot16(solved, slab[k, rows, j : j + tile])
+                    block = jnp.concatenate([slab[k, rows_of, j : j + tile] for rows_of in rows], axis=0)
+                    block = dot16(solved, block)
                     if order == 0:
                         mixed[k, :, j : j + tile] = block
                     else:
@@ -361,12 +357,28 @@
 
         cols = [jnp.broadcast_to(hour_cols[:, k : k + 1], (rank, 128)) for k in range(hours)]
         for s in range(n_smp):
-            block = cols[0] * mixed[0, :, s * 128 : (s + 1) * 128]
+            at = place(s) * 128
+            block = cols[0] * mixed[0, :, at : at + 128]
             for k in range(1, hours):
-                block = block + cols[k] * mixed[k, :, s * 128 : (s + 1) * 128]
+                block = block + cols[k] * mixed[k, :, at : at + 128]
             rs2_send[s] = block.astype(rs2_send.dtype)
         rs2_recv[smp] = rs2_send[smp]
         start_exchange("smp", lambda peer: rs2_send.at[peer], rs2_recv.at[smp], lambda step: RS2)
+
+        message = pack(gram_part + dot16(solved, solved, NT))
+        gs_send[...] = message
+        gs_recv[smp] = message
+        start_exchange("smp", lambda peer: gs_send, gs_recv.at[smp], lambda step: GS)
+
+        finish_exchange(RS2, rs2_recv.at[pl.ds(0, n_smp - 1)])
+        total = rs2_recv[0].astype(jnp.float32)
+        for s in range(1, n_smp):
+            total = total + rs2_recv[s].astype(jnp.float32)
+        b_slice[...] = total
+        message = total.astype(jnp.bfloat16)
+        ag2_send[...] = message
+        ag2_recv[smp] = message
+        start_exchange("smp", lambda peer: ag2_send, ag2_recv.at[smp], lambda step: AG2 + step[1])
 
         finish_exchange(GS, gs_recv.at[pl.ds(0, n_smp - 1)])
         gram_raw = gs_recv[0]
@@ -378,17 +390,8 @@
         inv_s_col[...] = jnp.broadcast_to(inv_col, inv_s_col.shape)
         gram_sample[...] = gram_raw * (inv_col * inv_row)
         inverse = regularized_inverse(gram_sample[...] * gram_hour) * inv_row
-
-        finish_exchange(RS2, rs2_recv.at[pl.ds(0, n_smp - 1)])
-        total = rs2_recv[0].astype(jnp.float32)
-        for s in range(1, n_smp):
-            total = total + rs2_recv[s].astype(jnp.float32)
-        unscaled = product_two_parts(inverse, total)
-        ub_slice[...] = unscaled
-        message = unscaled.astype(jnp.bfloat16)
-        ag2_send[...] = message
-        ag2_recv[smp] = message
-        start_exchange("smp", lambda peer: ag2_send, ag2_recv.at[smp], lambda step: AG2 + step[1])
+        inv_build[...] = inverse
+        parts = jnp.concatenate(low16(*split(inverse)), axis=0)[:, :rank]
 
         sums = [jnp.zeros((rank, 128), jnp.float32) for _ in range(hours)]
         gram_part = jnp.zeros((rank, rank), jnp.float32)
@@ -398,7 +401,8 @@
         for order, dz in enumerate((0, 1, 3, 2)):
             finish_exchange(AG2 + dz, ag2_recv.at[pl.ds(0, 1 if dz == 0 else 2)])
             group = groups[order]
-            solved = gathered([group])
+            solved = solve_columns(parts, gathered(group))
+            factor[:, pl.ds(pl.multiple_of(group * 256, 256), 256)] = solved
             gram_part = gram_part + dot16(solved, solved, NT)
             wide = solved.astype(jnp.float32)
             for k in range(hours):
@@ -448,10 +452,11 @@
                 pair_finish(k - 1)
             pair_finish(hours - 1)
 
-        finish_exchange(P1, p1_recv.at[pl.ds(0, n_bld - 1)])
+        rows = p1_recv.shape[0]
+        finish_exchange(P1, p1_recv.at[pl.ds(0, rows - 1)])
         total = p1_recv[0]
-        for b in range(1, n_bld):
-            total = total + p1_recv[b]
+        for n in range(1, rows):
+            total = total + p1_recv[n]
         p2_send[...] = total
         p2_recv[smp] = total
         start_exchange("smp", lambda peer: p2_send, p2_recv.at[smp], lambda step: P2)
@@ -465,10 +470,11 @@
         one, two = left_parts(inverse)
         scale_row = inv_row * inv_s_row[0:1, :]
 
-        finish_exchange(P2, p2_recv.at[pl.ds(0, n_smp - 1)])
+        planes = p2_recv.shape[0]
+        finish_exchange(P2, p2_recv.at[pl.ds(0, planes - 1)])
         total = p2_recv[0]
-        for s in range(1, n_smp):
-            total = total + p2_recv[s]
+        for n in range(1, planes):
+            total = total + p2_recv[n]
         right = total * scale_row
         hour_rhs[...] = right
         high, middle, rest = split(right)
@@ -478,7 +484,7 @@
         hour_cols[...] = dot16(one, jnp.concatenate([both, far], axis=1), NT) + dot16(two, both, NT)
 
     sample_out[...] = product(inv_sample[...], unpack_twice(s_slice[...]))[:, :rank] * inv_s_col[:, 0:1]
-    build_out[...] = ub_slice[...] * inv_b_col[:, 0:1]
+    build_out[...] = product(inv_build[...], b_slice[...]) * inv_b_col[:, 0:1]
     hour_out[...] = dot32(hour_rhs[:, 0:rank], inv_hour[:, 0:rank])[0:hours] * scale_up
 
 
@@ -516,6 +522,7 @@
             pltpu.VMEM((hours, n_i, n_j), bf16),
             pltpu.VMEM((hours, rank, n_j), f32),
             pltpu.VMEM((hours, rank, n_i), f32),
+            pltpu.VMEM((rank, n_j), bf16),
             pltpu.VMEM((hours, n_bld // 2, rank // 2, 2 * i_share), f32),
             pltpu.VMEM((hours, n_bld // 2, rank // 2, 2 * i_share), bf16),
             pltpu.VMEM((hours, n_bld // 2, rank // 2, 2 * i_share), bf16),
@@ -523,6 +530,7 @@
             pltpu.VMEM((rank // 2, 2 * rank), f32),
             pltpu.VMEM((rank // 2, 2 * i_share), f32),
             pltpu.VMEM((rank, j_share), f32),
+            pltpu.VMEM((rank, 2 * rank), f32),
             pltpu.VMEM((rank, 2 * rank), f32),
             pltpu.VMEM((rank, 2 * rank), f32),
             pltpu.VMEM((rank, 2 * rank), f32),
@@ -550,7 +558,7 @@
             pltpu.VMEM((n_bld, pad, 2 * rank), f32),
             pltpu.VMEM((pad, 2 * rank), f32),
             pltpu.VMEM((n_smp, pad, 2 * rank), f32),
-            pltpu.SemaphoreType.DMA((hours,)),
+            pltpu.SemaphoreType.DMA((hours, n_smp)),
             pltpu.SemaphoreType.DMA((COUNT,)),
             pltpu.SemaphoreType.DMA((COUNT,)),
         ],

time: 157 us -> 152 us (0.968)
  Pallas kernels: 156 us -> 151 us
    pallas_call x1, Pallas kernels: 155 us -> 149 us  [local(): pl.pallas_call(body, out_shape=(jax.ShapeDtypeStruct((rank, i_share), f32...]
where the time goes in v5:
time: 152 us
  Pallas kernels  151 us (99%)
    pallas_call x1, Pallas kernels, local(): pl.pallas_call(body, out_shape=(jax.ShapeDtypeStruct((rank, i_share), f32...  149 us

profile of v5, /device:TPU:1, one launch (start us, length us, event | category | flops | bytes accessed | tf_op | source)
XLA Modules:
  0.0 151.5 jit_solution(9299557835168376361)
XLA Ops:
  0.6 149.4 %als_sweeps.1 = (f32[64,64]{1,0:T(8,128)}, f32[64,128]{1,0:T(8,128)}, f32[4,64]{1,0:T(4,128)}) custom-call(bf16[4,1024,1024]{2,1,0:T(8,128)(2,1)} %tensor_ref.1, f32[64,1024]{1,0:T(8,128)} %build_ref.1, f32[4,64]{1,0:T(4,128)} %hour_ref.1), custom_call_target="tpu_custom_call" | custom-call | tf_op jit(solution)/shard_map/als_sweeps/pallas_call | solution.py:512
  150.1 1.4 put_out.1

commit v6 on v5

--- a/solution.py
+++ b/solution.py
@@ -397,7 +397,7 @@
         gram_part = jnp.zeros((rank, rank), jnp.float32)
         before_last = sweep < SWEEPS - 1
         groups = [(z - dz + 4) % 4 for dz in (0, 1, 3, 2)]
-        early = {k: groups[:2] if k < 2 else groups[:1] for k in range(hours)}
+        early = {k: groups[:1] for k in range(hours)}
         for order, dz in enumerate((0, 1, 3, 2)):
             finish_exchange(AG2 + dz, ag2_recv.at[pl.ds(0, 1 if dz == 0 else 2)])
             group = groups[order]

time: 152 us -> 149 us (0.980)
  Pallas kernels: 151 us -> 148 us
    pallas_call x1, Pallas kernels: 149 us -> 147 us  [local(): pl.pallas_call(body, out_shape=(jax.ShapeDtypeStruct((rank, i_share), f32...]
where the time goes in v6:
time: 149 us
  Pallas kernels  148 us (99%)
    pallas_call x1, Pallas kernels, local(): pl.pallas_call(body, out_shape=(jax.ShapeDtypeStruct((rank, i_share), f32...  147 us

profile of v6, /device:TPU:1, one launch (start us, length us, event | category | flops | bytes accessed | tf_op | source)
XLA Modules:
  0.0 148.8 jit_solution(17517209999016877795)
XLA Ops:
  0.6 146.7 %als_sweeps.1 = (f32[64,64]{1,0:T(8,128)}, f32[64,128]{1,0:T(8,128)}, f32[4,64]{1,0:T(4,128)}) custom-call(bf16[4,1024,1024]{2,1,0:T(8,128)(2,1)} %tensor_ref.1, f32[64,1024]{1,0:T(8,128)} %build_ref.1, f32[4,64]{1,0:T(4,128)} %hour_ref.1), custom_call_target="tpu_custom_call" | custom-call | tf_op jit(solution)/shard_map/als_sweeps/pallas_call | solution.py:512
  147.3 1.4 put_out.1

commit v7 on v6

--- a/solution.py
+++ b/solution.py
@@ -397,7 +397,7 @@
         gram_part = jnp.zeros((rank, rank), jnp.float32)
         before_last = sweep < SWEEPS - 1
         groups = [(z - dz + 4) % 4 for dz in (0, 1, 3, 2)]
-        early = {k: groups[:1] for k in range(hours)}
+        early = {k: groups[:1] if k < 2 else [] for k in range(hours)}
         for order, dz in enumerate((0, 1, 3, 2)):
             finish_exchange(AG2 + dz, ag2_recv.at[pl.ds(0, 1 if dz == 0 else 2)])
             group = groups[order]
@@ -408,7 +408,7 @@
             for k in range(hours):
                 terms = slices(mixed, (k, slice(None)), [group]) * wide
                 sums[k] = sums[k] + (terms[:, :128] + terms[:, 128:])
-            if order < 2:
+            if order < 1:
 
                 @pl.when(before_last)
                 def _():
@@ -432,7 +432,8 @@
         def finish_project(k):
             left = groups[len(early[k]) :]
             for i in range(0, n_i, tile):
-                scatter(k, i, partial[k, :, i : i + tile] + project(k, i, left))
+                block = project(k, i, left)
+                scatter(k, i, partial[k, :, i : i + tile] + block if early[k] else block)
             pair_start(k)
 
         @pl.when(before_last)

time: 149 us -> 148 us (level)
  no operation moved by 1% of the time
where the time goes in v7:
time: 148 us
  Pallas kernels  147 us (99%)
    pallas_call x1, Pallas kernels, local(): pl.pallas_call(body, out_shape=(jax.ShapeDtypeStruct((rank, i_share), f32...  146 us

profile of v7, /device:TPU:1, one launch (start us, length us, event | category | flops | bytes accessed | tf_op | source)
XLA Modules:
  0.0 148.0 jit_solution(17779344661704148268)
XLA Ops:
  0.6 145.9 %als_sweeps.1 = (f32[64,64]{1,0:T(8,128)}, f32[64,128]{1,0:T(8,128)}, f32[4,64]{1,0:T(4,128)}) custom-call(bf16[4,1024,1024]{2,1,0:T(8,128)(2,1)} %tensor_ref.1, f32[64,1024]{1,0:T(8,128)} %build_ref.1, f32[4,64]{1,0:T(4,128)} %hour_ref.1), custom_call_target="tpu_custom_call" | custom-call | tf_op jit(solution)/shard_map/als_sweeps/pallas_call | solution.py:513
  146.6 1.4 put_out.1
